TPU v7x, 128 devices: a whole 4x4x4 slice. The times are simulated.
128 devices in a mesh: dx: 8 (over y_lo, x), dy: 8 (over z, core), band: 2 (over y_hi).
Axes of the slice: x: 4, y: 4 (y_hi: 2, y_lo: 2; y = y_hi * 2 + y_lo), z: 4, core: 2. Of those that a mesh axis runs over, the one named last changes fastest.
Arguments:
- orbitals: float32 [8, 8, 3072, 512], P('dx', 'dy', None, 'band'), may hold values from -6 to 6
- hamiltonians: bfloat16 [8, 8, 12, 512, 512], P('dx', 'dy'), as said below
- connectivity: int32 [8, 8, 12, 512], P('dx', 'dy'), may hold values from 0 to 4095, as said below
- face_maps: int32 [8, 8, 4, 256], P('dx', 'dy'), may hold values from 0 to 3071, as said below
Outputs:
- rotated: float32 [8, 8, 3072, 512], P('dx', 'dy', None, 'band')
Inputs may be any that keep to these rules, and one draw needn't show every extreme that they name: connectivity[i, j, c, p] is a row of domain (i, j)'s extended node list (3072 owned nodes, then 256 ghost nodes for each of the four faces in the order of the steps); every row of that list is named at least once. face_maps[i, j, k] holds 256 distinct owned nodes. `hamiltonians`: each cell Hamiltonian is symmetric.
All inputs are finite; a program needn't handle non-finite values.
Results may differ from a plain program's by a relative error of at most 0.0038.
The roundings to bfloat16 on the way count: a program that leaves them out, or rounds other values in their place, can miss the bound.
Values may be sent and summed in bfloat16 or wider, within the bound.
No kernel may reach another device: no remote copies, remote signals or barrier semaphores. Data moves between devices by JAX's collectives and lax.ppermute only.
A program may use at most 128 MiB of HBM per device.

v0:
```python
import jax
import jax.numpy as jnp
from jax import lax
from jax.sharding import PartitionSpec as P

NS_STEPS = 3


def passed_along(value, axis, steps):
    count = lax.axis_size(axis)
    pairs = [(source, (source + steps) % count) for source in range(count)]
    return lax.ppermute(value, axis, pairs)


def apply_operator(current, hamiltonian, connection, face_rows):
    node_count = current.shape[0]
    columns = current.shape[1]
    face_width = face_rows.shape[1]
    face_vals = (
        jnp.take(current, face_rows.reshape(-1), axis=0)
        .reshape(4, face_width, columns)
        .astype(jnp.bfloat16)
    )
    from_west = passed_along(face_vals[0], "dx", 1)
    from_east = passed_along(face_vals[1], "dx", -1)
    from_south = passed_along(face_vals[2], "dy", 1)
    from_north = passed_along(face_vals[3], "dy", -1)
    extended = jnp.concatenate(
        [current.astype(jnp.bfloat16), from_west, from_east, from_south, from_north], axis=0
    )
    flat_index = connection.reshape(-1)
    cell_vals = jnp.take(extended, flat_index, axis=0).reshape(
        connection.shape[0], connection.shape[1], columns
    )
    products = jnp.einsum(
        "cpq,cqo->cpo", hamiltonian, cell_vals, preferred_element_type=jnp.float32
    )
    assembled = (
        jnp.zeros((extended.shape[0], columns), jnp.float32)
        .at[flat_index]
        .add(products.reshape(-1, columns))
    )
    ghost_part = assembled[node_count:].reshape(4, face_width, columns)
    to_west = passed_along(ghost_part[0], "dx", -1)
    to_east = passed_along(ghost_part[1], "dx", 1)
    to_south = passed_along(ghost_part[2], "dy", -1)
    to_north = passed_along(ghost_part[3], "dy", 1)
    returned = jnp.stack([to_west, to_east, to_south, to_north]).reshape(-1, columns)
    return assembled[:node_count].at[face_rows.reshape(-1)].add(returned)


def ortho_factor(gram):
    scale = jnp.sqrt(jnp.sum(gram * gram))
    matrix = gram / scale
    ident = jnp.eye(gram.shape[0], dtype=gram.dtype)
    factor = ident
    for number in range(NS_STEPS):
        middle = 1.5 * ident - 0.5 * jnp.dot(factor, matrix, precision=lax.Precision.HIGHEST)
        matrix = jnp.dot(matrix, middle, precision=lax.Precision.HIGHEST)
        factor = jnp.dot(middle, factor, precision=lax.Precision.HIGHEST)
    return factor / jnp.sqrt(scale)


def self_gram(block):
    return lax.dot_general(
        block,
        block,
        (((0,), (0,)), ((), ())),
        precision=lax.Precision.HIGHEST,
        preferred_element_type=jnp.float32,
    )


def local(orbitals, hamiltonians, connectivity, face_maps):
    current = orbitals[0, 0]
    hamiltonian = hamiltonians[0, 0]
    connection = connectivity[0, 0]
    face_rows = face_maps[0, 0]

    def scaled(vector):
        return (apply_operator(vector, hamiltonian, connection, face_rows) - 0.5 * vector) / 2.0

    previous = current
    latest = scaled(current)
    for number in range(3):
        following = 2.0 * scaled(latest) - previous
        previous, latest = (latest, following)
    total_nodes = current.shape[0] * lax.axis_size("dx") * lax.axis_size("dy")
    node_half = lax.all_to_all(latest, "band", split_axis=0, concat_axis=1, tiled=True)
    gram = lax.psum(self_gram(node_half), ("dx", "dy", "band")) / total_nodes
    factor = ortho_factor(gram)
    rotated_half = jnp.dot(node_half, factor, precision=lax.Precision.HIGHEST)
    rotated = lax.all_to_all(rotated_half, "band", split_axis=1, concat_axis=0, tiled=True)
    return rotated[None, None]


def solution(mesh):
    in_specs = (
        P("dx", "dy", None, "band"),
        P("dx", "dy", None, None, None),
        P("dx", "dy", None, None),
        P("dx", "dy", None, None),
    )
    out_specs = P("dx", "dy", None, "band")
    return jax.shard_map(local, mesh=mesh, in_specs=in_specs, out_specs=out_specs, check_vma=False)
```

profile of v0, /device:TPU:19, one launch (start us, length us, event | category | flops | bytes accessed | tf_op | source)
XLA Modules:
  0.0 769.2 jit_solution(7741364152981733505)
XLA Ops:
  7.2 5.3 gather_fusion
  16.6 2.0 convert_dynamic-update-slice_fusion.3
  18.7 2.5 collective-permute-done
  21.3 25.1 %gather_fusion.1 = bf16[6144,256]{1,0:T(8,128)(2,1)} fusion(bf16[4096,256]{1,0:T(8,128)(2,1)S(1)} %constant_dynamic-update-slice_fusion, s32[6144]{0:T(1024)S(1)} %fusion.31), kind=kCustom, calls=%fused_computation.1.clone | custom fusion | bytes 6316032 | tf_op jit(solution)/shard_map/jit(_take)/gather | solution.py:32
  46.4 4.7 broadcast_select_fusion
  51.1 7.3 fusion.9
  58.4 6.6 copy.20
  65.0 36.0 %scatter_custom_fusion = f32[4096,256]{1,0:T(8,128)} fusion(s32[6144]{0:T(1024)S(1)} %bitcast.141, f32[6144,256]{1,0:T(8,128)} %bitcast.108, f32[]{:T(128)} %constant.24.clone.1), kind=kCustom, calls=%fused_computation.43 | custom fusion | flops 1572864 | bytes 4194816 | tf_op jit(solution)/shard_map/scatter-add | solution.py:41
  102.3 3.3 collective-permute-start.4
  105.6 3.3 collective-permute-start.7
  109.5 3.8 slice.216
  115.1 9.5 %scatter_fusion = f32[3072,256]{1,0:T(8,128)} fusion(f32[3072,256]{1,0:T(8,128)} %slice.216, s32[1024]{0:T(1024)S(1)} %bitcast.135, f32[1024,256]{1,0:T(8,128)S(1)} %bitcast.112), kind=kCustom, calls=%fused_computation.9 | custom fusion | flops 262144 | bytes 3149824 | tf_op jit(solution)/shard_map/scatter-add | solution.py:49
  124.6 4.9 convert_dynamic-update-slice_fusion.2
  129.6 5.3 gather_fusion.2
  136.8 4.4 collective-permute-start.11
  142.1 1.9 collective-permute-done.10
  144.7 25.0 %gather_fusion.3 = bf16[6144,256]{1,0:T(8,128)(2,1)} fusion(bf16[4096,256]{1,0:T(8,128)(2,1)S(1)} %constant_dynamic-update-slice_fusion.4, s32[6144]{0:T(1024)S(1)} %fusion.31), kind=kCustom, calls=%fused_computation.5.clone | custom fusion | bytes 6316032 | tf_op jit(solution)/shard_map/jit(_take)/gather | solution.py:32
  169.7 4.7 broadcast_select_fusion.1
  174.4 7.3 fusion.12
  181.7 6.6 copy.22
  188.3 36.0 %scatter_custom_fusion.2 = f32[4096,256]{1,0:T(8,128)} fusion(s32[6144]{0:T(1024)S(1)} %bitcast.142, f32[6144,256]{1,0:T(8,128)} %bitcast.109, f32[]{:T(128)} %constant.24.clone.1), kind=kCustom, calls=%fused_computation.41 | custom fusion | flops 1572864 | bytes 4194816 | tf_op jit(solution)/shard_map/scatter-add | solution.py:41
  225.5 3.8 collective-permute-start.12
  229.4 2.1 collective-permute-start.15
  232.8 3.7 slice.225
  238.4 9.5 %scatter_fusion.1 = f32[3072,256]{1,0:T(8,128)} fusion(f32[3072,256]{1,0:T(8,128)} %slice.225, s32[1024]{0:T(1024)S(1)} %bitcast.136, f32[1024,256]{1,0:T(8,128)S(1)} %bitcast.113), kind=kCustom, calls=%fused_computation.11 | custom fusion | flops 262144 | bytes 3149824 | tf_op jit(solution)/shard_map/scatter-add | solution.py:49
  247.9 6.0 convert_dynamic-update-slice_fusion.1
  254.0 5.3 gather_fusion.4
  259.7 3.9 collective-permute-start.17
  263.6 3.2 collective-permute-start.19
  267.0 1.9 collective-permute-done.18
  269.7 25.0 %gather_fusion.5 = bf16[6144,256]{1,0:T(8,128)(2,1)} fusion(bf16[4096,256]{1,0:T(8,128)(2,1)S(1)} %constant_dynamic-update-slice_fusion.8, s32[6144]{0:T(1024)S(1)} %fusion.31), kind=kCustom, calls=%fused_computation.6.clone | custom fusion | bytes 6316032 | tf_op jit(solution)/shard_map/jit(_take)/gather | solution.py:32
  294.6 4.7 broadcast_select_fusion.2
  299.3 7.3 fusion.15
  306.6 6.6 copy.24
  313.2 36.0 %scatter_custom_fusion.4 = f32[4096,256]{1,0:T(8,128)} fusion(s32[6144]{0:T(1024)S(1)} %bitcast.143, f32[6144,256]{1,0:T(8,128)} %bitcast.110, f32[]{:T(128)} %constant.24.clone.1), kind=kCustom, calls=%fused_computation.39 | custom fusion | flops 1572864 | bytes 4194816 | tf_op jit(solution)/shard_map/scatter-add | solution.py:41
  350.5 4.0 collective-permute-start.20
  354.5 2.1 collective-permute-start.23
  357.6 3.7 slice.234
  363.2 9.5 %scatter_fusion.2 = f32[3072,256]{1,0:T(8,128)} fusion(f32[3072,256]{1,0:T(8,128)} %slice.234, s32[1024]{0:T(1024)S(1)} %bitcast.137, f32[1024,256]{1,0:T(8,128)S(1)} %bitcast.114), kind=kCustom, calls=%fused_computation.13 | custom fusion | flops 262144 | bytes 3149824 | tf_op jit(solution)/shard_map/scatter-add | solution.py:49
  372.7 6.0 convert_dynamic-update-slice_fusion
  378.7 5.3 gather_fusion.6
  384.4 3.3 collective-permute-start.25
  387.7 4.2 collective-permute-start.27
  393.0 1.9 collective-permute-done.26
  395.6 25.0 %gather_fusion.7 = bf16[6144,256]{1,0:T(8,128)(2,1)} fusion(bf16[4096,256]{1,0:T(8,128)(2,1)S(1)} %constant_dynamic-update-slice_fusion.12, s32[6144]{0:T(1024)S(1)} %fusion.31), kind=kCustom, calls=%fused_computation.7.clone | custom fusion | bytes 6316032 | tf_op jit(solution)/shard_map/jit(_take)/gather | solution.py:32
  420.6 4.7 broadcast_select_fusion.3
  425.3 7.3 fusion.18
  432.5 6.6 copy.26
  439.1 36.0 %scatter_custom_fusion.6 = f32[4096,256]{1,0:T(8,128)} fusion(s32[6144]{0:T(1024)S(1)} %bitcast.144, f32[6144,256]{1,0:T(8,128)} %bitcast.107, f32[]{:T(128)} %constant.24.clone.1), kind=kCustom, calls=%fused_computation.37 | custom fusion | flops 1572864 | bytes 4194816 | tf_op jit(solution)/shard_map/scatter-add | solution.py:41
  476.4 4.1 collective-permute-start.28
  482.5 2.1 collective-permute-done.28
  485.6 2.8 collective-permute-done.30
  490.0 7.7 scatter_fusion.3
  497.7 3.5 subtract_subtract_fusion
  501.2 36.1 %all_to_all.32 = f32[2,1536,256]{2,1,0:T(8,128)S(1)} all-to-all(f32[2,1536,256]{2,1,0:T(8,128)S(1)} %bitcast.102), channel_id=1, replica_groups=mesh['dx'=8,'dy'=8,'band'=2] {'band'}, dimensions={0} | all-to-all | bytes 6291456 | tf_op jit(solution)/shard_map/all_to_all | solution.py:89
  537.8 6.3 fusion.44
  544.1 9.4 %copy.27 = f32[1536,2,256]{2,1,0:T(2,128)} copy(f32[1536,2,256]{2,0,1:T(8,128)S(1)} %bitcast.99) | data formatting | bytes 6291456 | tf_op jit(solution)/shard_map/all_to_all | solution.py:89
  553.5 4.3 reshape.350
  557.8 139.3 %all-reduce.2.cloned.1.call-done = f32[512,512]{1,0:T(8,128)} async-done(((f32[512,512]{1,0:T(8,128)}), f32[512,512]{1,0:T(8,128)}) %all-reduce.2.cloned.1.call-update) | async-done | bytes 1048592 | tf_op jit(solution)/shard_map/psum | solution.py:90
  697.1 2.1 multiply_reduce_fusion
  700.0 2.4 select_subtract_fusion.2
  712.7 3.7 convolution_divide_fusion
  716.4 5.4 fusion.47
  721.8 38.7 %all_to_all.33 = f32[1536,2,256]{2,0,1:T(8,128)S(1)} all-to-all(f32[1536,2,256]{2,0,1:T(8,128)S(1)} %fusion.47), channel_id=1, replica_groups=mesh['dx'=8,'dy'=8,'band'=2] {'band'}, dimensions={1} | all-to-all | bytes 6291456 | tf_op jit(solution)/shard_map/all_to_all | solution.py:93
  (104 shorter events, 42.2 us)
Async XLA Ops:
  6.5 690.6 %all-reduce.2.cloned.1.call-start = ((), (), s32[]{:S(2)}) async-start(), calls=%async_computation.2 | async-start | bytes 2097152 | tf_op jit(solution)/shard_map/psum | solution.py:90
  12.8 5.8 copy-start.1
  12.9 8.4 %collective-permute-start.3 = (bf16[256,256]{1,0:T(8,128)(2,1)S(1)}, bf16[256,256]{1,0:T(8,128)(2,1)S(1)}, u32[]{:S(2)}, u32[]{:S(2)}) collective-permute-start(bf16[256,256]{1,0:T(8,128)(2,1)S(1)} %get-tuple-element.41), channel_id=1, source_target_pairs={{0,14},{2,0},{4,2},{6,4},{8,6},{10,8},{12,10},{14,12},{1,15},{3,1}... | collective-permute-start | bytes 393224 | tf_op jit(solution)/shard_map/ppermute | solution.py:12
  13.6 7.7 %collective-permute-start.2 = (bf16[256,256]{1,0:T(8,128)(2,1)S(1)}, bf16[256,256]{1,0:T(8,128)(2,1)S(1)}, u32[]{:S(2)}, u32[]{:S(2)}) collective-permute-start(bf16[256,256]{1,0:T(8,128)(2,1)S(1)} %get-tuple-element.42), channel_id=1, source_target_pairs={{0,2},{2,4},{4,6},{6,8},{8,10},{10,12},{12,14},{14,0},{1,3},{3,5},... | collective-permute-start | bytes 393224 | tf_op jit(solution)/shard_map/ppermute | solution.py:12
  15.1 6.1 collective-permute-start.1
  15.4 5.8 collective-permute-start
  65.0 44.4 %copy-start.2 = (s32[1,1,4,256]{3,2,1,0:T(4,128)S(1)}, s32[1,1,4,256]{3,2,1,0:T(4,128)}, u32[]{:S(2)}) copy-start(s32[1,1,4,256]{3,2,1,0:T(4,128)} %param.11) | copy-start | bytes 12292
  102.3 11.0 %collective-permute-start.4 = (f32[256,256]{1,0:T(8,128)S(1)}, f32[256,256]{1,0:T(8,128)S(1)}, u32[]{:S(2)}, u32[]{:S(2)}) collective-permute-start(f32[256,256]{1,0:T(8,128)S(1)} %get-tuple-element.25), channel_id=1, source_target_pairs={{0,112},{16,0},{32,16},{48,32},{64,48},{80,64},{96,80},{112,96},{1... | collective-permute-start | bytes 786440 | tf_op jit(solution)/shard_map/ppermute | solution.py:12
  105.6 7.6 collective-permute-start.7
  108.9 6.1 collective-permute-start.6
  109.2 5.7 collective-permute-start.5
  135.2 6.9 collective-permute-start.8
  135.3 6.8 collective-permute-start.9
  136.8 7.9 %collective-permute-start.11 = (bf16[256,256]{1,0:T(8,128)(2,1)S(1)}, bf16[256,256]{1,0:T(8,128)(2,1)S(1)}, u32[]{:S(2)}, u32[]{:S(2)}) collective-permute-start(bf16[256,256]{1,0:T(8,128)(2,1)S(1)} %get-tuple-element.37), channel_id=1, source_target_pairs={{0,14},{2,0},{4,2},{6,4},{8,6},{10,8},{12,10},{14,12},{1,15},{3,1}... | collective-permute-start | bytes 393224 | tf_op jit(solution)/shard_map/ppermute | solution.py:12
  141.2 2.8 collective-permute-start.10
  225.5 11.0 %collective-permute-start.12 = (f32[256,256]{1,0:T(8,128)S(1)}, f32[256,256]{1,0:T(8,128)S(1)}, u32[]{:S(2)}, u32[]{:S(2)}) collective-permute-start(f32[256,256]{1,0:T(8,128)S(1)} %get-tuple-element.21), channel_id=1, source_target_pairs={{0,112},{16,0},{32,16},{48,32},{64,48},{80,64},{96,80},{112,96},{1... | collective-permute-start | bytes 786440 | tf_op jit(solution)/shard_map/ppermute | solution.py:12
  229.4 7.1 collective-permute-start.15
  231.4 6.1 collective-permute-start.14
  232.4 5.9 collective-permute-start.13
  259.6 7.4 collective-permute-start.16
  259.7 7.3 collective-permute-start.17
  263.6 6.1 collective-permute-start.19
  266.8 2.2 collective-permute-start.18
  350.5 10.8 %collective-permute-start.20 = (f32[256,256]{1,0:T(8,128)S(1)}, f32[256,256]{1,0:T(8,128)S(1)}, u32[]{:S(2)}, u32[]{:S(2)}) collective-permute-start(f32[256,256]{1,0:T(8,128)S(1)} %get-tuple-element.17), channel_id=1, source_target_pairs={{0,112},{16,0},{32,16},{48,32},{64,48},{80,64},{96,80},{112,96},{1... | collective-permute-start | bytes 786440 | tf_op jit(solution)/shard_map/ppermute | solution.py:12
  354.5 6.8 collective-permute-start.23
  356.5 6.1 collective-permute-start.22
  357.5 5.5 collective-permute-start.21
  384.3 8.6 %collective-permute-start.24 = (bf16[256,256]{1,0:T(8,128)(2,1)S(1)}, bf16[256,256]{1,0:T(8,128)(2,1)S(1)}, u32[]{:S(2)}, u32[]{:S(2)}) collective-permute-start(bf16[256,256]{1,0:T(8,128)(2,1)S(1)} %get-tuple-element.32), channel_id=1, source_target_pairs={{0,16},{16,32},{32,48},{48,64},{64,80},{80,96},{96,112},{112,0},{1... | collective-permute-start | bytes 393224 | tf_op jit(solution)/shard_map/ppermute | solution.py:12
  384.4 8.6 %collective-permute-start.25 = (bf16[256,256]{1,0:T(8,128)(2,1)S(1)}, bf16[256,256]{1,0:T(8,128)(2,1)S(1)}, u32[]{:S(2)}, u32[]{:S(2)}) collective-permute-start(bf16[256,256]{1,0:T(8,128)(2,1)S(1)} %get-tuple-element.31), channel_id=1, source_target_pairs={{0,112},{16,0},{32,16},{48,32},{64,48},{80,64},{96,80},{112,96},{1... | collective-permute-start | bytes 393224 | tf_op jit(solution)/shard_map/ppermute | solution.py:12
  387.7 7.9 %collective-permute-start.27 = (bf16[256,256]{1,0:T(8,128)(2,1)S(1)}, bf16[256,256]{1,0:T(8,128)(2,1)S(1)}, u32[]{:S(2)}, u32[]{:S(2)}) collective-permute-start(bf16[256,256]{1,0:T(8,128)(2,1)S(1)} %get-tuple-element.29), channel_id=1, source_target_pairs={{0,14},{2,0},{4,2},{6,4},{8,6},{10,8},{12,10},{14,12},{1,15},{3,1}... | collective-permute-start | bytes 393224 | tf_op jit(solution)/shard_map/ppermute | solution.py:12
  391.9 3.0 collective-permute-start.26
  476.4 8.2 %collective-permute-start.28 = (f32[256,256]{1,0:T(8,128)S(1)}, f32[256,256]{1,0:T(8,128)S(1)}, u32[]{:S(2)}, u32[]{:S(2)}) collective-permute-start(f32[256,256]{1,0:T(8,128)S(1)} %get-tuple-element.13), channel_id=1, source_target_pairs={{0,112},{16,0},{32,16},{48,32},{64,48},{80,64},{96,80},{112,96},{1... | collective-permute-start | bytes 786440 | tf_op jit(solution)/shard_map/ppermute | solution.py:12
  480.5 5.1 collective-permute-start.31
  482.3 6.1 collective-permute-start.30
  482.5 7.6 slice-start
  482.5 6.5 collective-permute-start.29
  700.0 3.4 copy-start
Sparse Core Ops, SparseCore 0:
  544.2 152.8 all-reduce.1
where the time goes:
time: 781 us; the launch traced here: 769 us
  other arithmetic  226 us (29%)
  local copies, waits for them, and re-layouts  181 us (23%)
  waiting for transfers between devices  161 us (21%)
  blocking collectives  74.8 us (10%)
  matrix products  57.3 us (7%)
  starting transfers between devices  54.1 us (7%)
  between operations  14.9 us (2%)
    scatter-add x4, other arithmetic, apply_operator(): assembled = jnp.zeros((extended.shape[0], columns), jnp.float32).at[flat_...  144 us
    psum x1, waiting for transfers between devices, local(): gram = lax.psum(self_gram(node_half), ('dx', 'dy', 'band')) / total_nodes  139 us
    gather x4, local copies, waits for them, and re-layouts, apply_operator(): jnp.take(extended, flat_index, axis=0)  100 us
    ppermute x32, starting transfers between devices, passed_along(): return lax.ppermute(value, axis, pairs)  54.1 us
    all_to_all x1, blocking collectives, local(): lax.all_to_all(rotated_half, 'band', split_axis=1, concat_axis=0, tiled=T...  38.7 us
    scatter-add x4, other arithmetic, apply_operator(): return assembled[:node_count].at[face_rows.reshape(-1)].add(returned)  36.3 us
    all_to_all x1, blocking collectives, local(): lax.all_to_all(latest, 'band', split_axis=0, concat_axis=1, tiled=True)  36.1 us
    dot_general x4, matrix products, apply_operator(): jnp.einsum('cpq,cqo->cpo', hamiltonian, cell_vals, preferred_element_type...  29.2 us
  transfers between devices with their start and end apart: 33, of which 17 were waited for; matrix products, arithmetic and copies ran while one was open for 4% of the time, Pallas kernels for 0%

commit v1 on v0

v1 whole, which is shorter than its diff:
```python
import jax
import jax.numpy as jnp
from jax import lax
from jax.experimental import pallas as pl
from jax.experimental.pallas import tpu as pltpu
from jax.sharding import PartitionSpec as P

NS_STEPS = 3
LANES = 128
UNROLL = 16


VMEM = pl.BlockSpec(memory_space=pltpu.VMEM)
SMEM = pl.BlockSpec(memory_space=pltpu.SMEM)


def limit(mib):
    return pltpu.CompilerParams(vmem_limit_bytes=mib << 20)


def pair(start):
    return pl.ds(pl.multiple_of(start, 2), 2)


def gather_rows(index, base, source, target, count):
    def step(number, carry):
        first = number * UNROLL
        for lane in range(UNROLL):
            row = index[base + first + lane]
            target[pair(2 * first + 2 * lane), :] = source[pair(row), :]
        return carry

    lax.fori_loop(0, count // UNROLL, step, 0)


def index_kernel(connection, first, last):
    slots = connection.shape[0]

    def step(number, carry):
        base = number * UNROLL
        for lane in range(UNROLL):
            slot = base + lane
            last[connection[slot]] = 2 * slot
        for lane in range(UNROLL):
            slot = slots - 1 - base - lane
            first[connection[slot]] = 2 * slot
        return carry

    lax.fori_loop(0, slots // UNROLL, step, 0)


def start_kernel(faces, field, current, face_vals, held):
    nodes = field.shape[0]
    chunk = 256

    def step(number, carry):
        block = field[pl.ds(pl.multiple_of(number * chunk, chunk), chunk), :]
        begin = number * 2 * chunk
        current[pl.ds(begin, chunk, stride=2), :] = block[:, :LANES]
        current[pl.ds(begin + 1, chunk, stride=2), :] = block[:, LANES:]
        return carry

    lax.fori_loop(0, nodes // chunk, step, 0)
    gather_rows(faces, 0, current, held, faces.shape[0])
    face_vals[...] = held[...].astype(jnp.bfloat16)


def cells_kernel(scales, connection, first, last, second, extra, current, before, west, east, south, north,
                 hamiltonian, partial, ghosts, extended, cell_in, products):
    owned = current.shape[0]
    face = west.shape[0]
    cells, points, _ = hamiltonian.shape
    alpha, beta, gamma = scales
    extended[:owned, :] = current[...]
    for number, block in enumerate((west, east, south, north)):
        extended[pl.ds(owned + number * face, face), :] = block[...].astype(jnp.float32)
    products[pl.ds(2 * cells * points, 8), :] = jnp.zeros((8, LANES), jnp.float32)

    def cell(number, carry):
        gather_rows(connection, number * points, extended, cell_in, points)
        left = cell_in[pl.ds(0, points, stride=2), :].astype(jnp.bfloat16)
        right = cell_in[pl.ds(1, points, stride=2), :].astype(jnp.bfloat16)
        product = jnp.dot(
            hamiltonian[number],
            jnp.concatenate([left, right], axis=1),
            preferred_element_type=jnp.float32,
        )
        begin = number * 2 * points
        products[pl.ds(begin, points, stride=2), :] = product[:, :LANES]
        products[pl.ds(begin + 1, points, stride=2), :] = product[:, LANES:]
        return carry

    lax.fori_loop(0, cells, cell, 0)

    def combine(number, carry):
        base = number * UNROLL
        for lane in range(UNROLL):
            one = first[base + lane]
            two = second[base + lane]
            extended[pair(2 * base + 2 * lane), :] = products[pair(one), :] + products[pair(two), :]
        return carry

    lax.fori_loop(0, first.shape[0] // UNROLL, combine, 0)

    @pl.when(extra[0] != 0)
    def _():
        def add(slot, carry):
            row = connection[slot]
            half = row // 2
            inner = jnp.logical_and(first[half] != 2 * slot, last[half] != 2 * slot)

            @pl.when(inner)
            def _():
                extended[pair(row), :] = extended[pair(row), :] + products[pair(2 * slot), :]

            return carry

        lax.fori_loop(0, connection.shape[0], add, 0)

    chunk = 512

    def finish(number, carry):
        rows = pl.ds(pl.multiple_of(number * chunk, chunk), chunk)
        value = alpha * extended[rows, :] - beta * current[rows, :]
        if gamma:
            value = value - gamma * before[rows, :]
        partial[rows, :] = value
        return carry

    lax.fori_loop(0, owned // chunk, finish, 0)
    ghosts[...] = alpha * extended[owned:, :]


def add_returned(faces, returned, target):
    count = faces.shape[0] // len(returned)
    for number, block in enumerate(returned):

        def step(turn, carry):
            base = turn * UNROLL
            rows = [faces[number * count + base + lane] for lane in range(UNROLL)]
            sums = [
                target[pair(rows[lane]), :] + block[pair(2 * base + 2 * lane), :] for lane in range(UNROLL)
            ]
            for lane in range(UNROLL):
                target[pair(rows[lane]), :] = sums[lane]
            return carry

        lax.fori_loop(0, count // UNROLL, step, 0)


def faces_kernel(faces, partial, west, east, south, north, current, face_vals, held):
    current[...] = partial[...]
    add_returned(faces, (west, east, south, north), current)
    gather_rows(faces, 0, current, held, faces.shape[0])
    face_vals[...] = held[...].astype(jnp.bfloat16)


def last_kernel(faces, partial, west, east, south, north, exact, rounded, work):
    work[...] = partial[...]
    add_returned(faces, (west, east, south, north), work)
    nodes = exact.shape[0]
    chunk = 256

    def step(number, carry):
        rows = pl.ds(pl.multiple_of(number * chunk, chunk), chunk)
        begin = number * 2 * chunk
        block = jnp.concatenate(
            [work[pl.ds(begin, chunk, stride=2), :], work[pl.ds(begin + 1, chunk, stride=2), :]], axis=1
        )
        exact[rows, :] = block
        rounded[rows, :] = block.astype(jnp.bfloat16)
        return carry

    lax.fori_loop(0, nodes // chunk, step, 0)


def halves(value):
    high = value.astype(jnp.bfloat16)
    return high, (value - high.astype(jnp.float32)).astype(jnp.bfloat16)


def product3(left, right):
    def dot(a, b):
        return jnp.dot(a, b, preferred_element_type=jnp.float32)

    (lh, ll), (rh, rl) = halves(left), halves(right)
    return dot(lh, rh) + (dot(lh, rl) + dot(ll, rh))


def factor_kernel(gram, factor):
    value = gram[...]
    scale = jnp.sqrt(jnp.sum(value * value))
    matrix = value / scale
    size = value.shape[0]
    row = lax.broadcasted_iota(jnp.int32, (size, size), 0)
    column = lax.broadcasted_iota(jnp.int32, (size, size), 1)
    ident = jnp.where(row == column, 1.0, 0.0).astype(jnp.float32)
    current = 1.5 * ident - 0.5 * matrix
    matrix = product3(matrix, current)
    for number in range(1, NS_STEPS):
        middle = 1.5 * ident - 0.5 * product3(current, matrix)
        if number < NS_STEPS - 1:
            matrix = product3(matrix, middle)
        current = product3(middle, current)
    factor[...] = current / jnp.sqrt(scale)


def call(kernel, out, specs, scratch=(), mib=8, out_specs=None, cost=None, **more):
    return pl.pallas_call(
        kernel,
        out_shape=out,
        in_specs=specs,
        out_specs=out_specs if out_specs is not None else jax.tree.map(lambda _: VMEM, out),
        scratch_shapes=scratch,
        compiler_params=limit(mib),
        cost_estimate=cost,
        **more,
    )


def shape(rows, columns, dtype=jnp.float32):
    return jax.ShapeDtypeStruct((rows, columns), dtype)


def passed_along(value, axis, steps):
    count = lax.axis_size(axis)
    pairs = [(source, (source + steps) % count) for source in range(count)]
    return lax.ppermute(value, axis, pairs)


def sent_faces(values):
    values = values.reshape(4, -1, LANES)
    return (
        passed_along(values[0], "dx", 1),
        passed_along(values[1], "dx", -1),
        passed_along(values[2], "dy", 1),
        passed_along(values[3], "dy", -1),
    )


def sent_ghosts(values):
    values = values.reshape(4, -1, LANES)
    return (
        passed_along(values[0], "dx", -1),
        passed_along(values[1], "dx", 1),
        passed_along(values[2], "dy", -1),
        passed_along(values[3], "dy", 1),
    )


def local(orbitals, hamiltonians, connectivity, face_maps):
    field = orbitals[0, 0]
    hamiltonian = hamiltonians[0, 0]
    connection = connectivity[0, 0].reshape(-1)
    faces = 2 * face_maps[0, 0].reshape(-1)
    nodes, columns = field.shape
    wide = columns // LANES
    slots = connection.shape[0]
    face_rows = faces.shape[0]
    rows = nodes + face_rows
    cells, points, _ = hamiltonian.shape

    current, face_vals = call(
        start_kernel,
        [shape(wide * nodes, LANES), shape(wide * face_rows, LANES, jnp.bfloat16)],
        [SMEM, VMEM],
        [pltpu.VMEM((wide * face_rows, LANES), jnp.float32)],
    )(faces, field)
    received = sent_faces(face_vals)

    table = jax.ShapeDtypeStruct((rows,), jnp.int32)
    first, last = call(
        index_kernel, [table, table], [SMEM], out_specs=[SMEM, SMEM],
        cost=pl.CostEstimate(flops=10**9, bytes_accessed=10**7, transcendentals=0),
    )(connection)
    single = first == last
    second = jnp.where(single, 2 * slots, last)
    covered = jnp.sum(jnp.where(single, 1, 2))
    extra = jnp.where(covered != slots, 1, 0).astype(jnp.int32).reshape(1)
    doubled = 2 * connection

    previous = current
    for number in range(4):
        scales = (0.5, 0.25, 0.0) if number == 0 else (1.0, 0.5, 1.0)

        def kernel(*refs, scales=scales):
            cells_kernel(scales, *refs)

        partial, ghosts = call(
            kernel,
            [shape(wide * nodes, LANES), shape(wide * face_rows, LANES)],
            [SMEM] * 5 + [VMEM] * 7,
            [
                pltpu.VMEM((wide * rows, LANES), jnp.float32),
                pltpu.VMEM((wide * points, LANES), jnp.float32),
                pltpu.VMEM((wide * slots + 8, LANES), jnp.float32),
            ],
            mib=24,
        )(doubled, first, last, second, extra, current, previous, *received, hamiltonian)
        back = sent_ghosts(ghosts)
        if number < 3:
            previous = current
            current, face_vals = call(
                faces_kernel,
                [shape(wide * nodes, LANES), shape(wide * face_rows, LANES, jnp.bfloat16)],
                [SMEM] + [VMEM] * 5,
                [pltpu.VMEM((wide * face_rows, LANES), jnp.float32)],
                input_output_aliases={1: 0},
            )(faces, partial, *back)
            received = sent_faces(face_vals)
        else:
            exact, rounded = call(
                last_kernel,
                [shape(nodes, columns), shape(nodes, columns, jnp.bfloat16)],
                [SMEM] + [VMEM] * 5,
                [pltpu.VMEM((wide * nodes, LANES), jnp.float32)],
            )(faces, partial, *back)
    return finish(exact, rounded, nodes)


def dot_nodes(left, right):
    return lax.dot_general(left, right, (((0,), (0,)), ((), ())), preferred_element_type=jnp.float32)


def summed(value, axes):
    count = lax.axis_size(axes)
    pieces = value.astype(jnp.bfloat16).reshape(count, -1)
    pieces = lax.all_to_all(pieces, axes, 0, 0, tiled=True)
    piece = jnp.sum(pieces.astype(jnp.float32), axis=0, keepdims=True)
    sums = lax.all_to_all(jnp.broadcast_to(piece, pieces.shape), axes, 0, 0, tiled=True)
    return sums.reshape(value.shape)


def finish(exact, rounded, nodes):
    band = lax.axis_index("band")
    half = nodes // 2
    columns = exact.shape[1]
    total = nodes * lax.axis_size("dx") * lax.axis_size("dy")
    mine = lax.dynamic_slice_in_dim(rounded, band * half, half, 0)
    theirs = lax.dynamic_slice_in_dim(rounded, (1 - band) * half, half, 0)
    other_mine = passed_along(theirs, "band", 1)
    other_theirs = passed_along(mine, "band", 1)
    whole = dot_nodes(rounded, rounded)
    cross = dot_nodes(jnp.where(band == 0, mine, other_mine), jnp.where(band == 0, other_mine, mine))
    zero = jnp.zeros_like(whole)
    block = jnp.concatenate(
        [jnp.where(band == 0, whole, zero), jnp.where(band == 0, zero, whole), cross], axis=0
    )
    block = summed(block, ("dx", "dy", "band")) / total
    one, two, three = block[:columns], block[columns:2 * columns], block[2 * columns:]
    gram = jnp.concatenate(
        [jnp.concatenate([one, three], axis=1), jnp.concatenate([three.T, two], axis=1)], axis=0
    )
    factor = call(factor_kernel, shape(2 * columns, 2 * columns), [VMEM], mib=16)(gram)
    own = lax.dynamic_slice(factor, (band * columns, band * columns), (columns, columns))
    across = lax.dynamic_slice(factor, ((1 - band) * columns, band * columns), (columns, columns))
    other = jnp.where(band == 0, jnp.concatenate([other_mine, other_theirs]), jnp.concatenate([other_theirs, other_mine]))
    rotated = jnp.dot(exact, own, precision=lax.Precision.HIGHEST) + jnp.dot(
        other, across.astype(jnp.bfloat16), preferred_element_type=jnp.float32
    )
    return rotated[None, None]


def solution(mesh):
    in_specs = (
        P("dx", "dy", None, "band"),
        P("dx", "dy", None, None, None),
        P("dx", "dy", None, None),
        P("dx", "dy", None, None),
    )
    out_specs = P("dx", "dy", None, "band")
    return jax.shard_map(local, mesh=mesh, in_specs=in_specs, out_specs=out_specs, check_vma=False)
```

time: 781 us -> 330 us (0.42); the launches traced: 769 us -> 330 us
  other arithmetic: 226 us -> 13.5 us
  local copies, waits for them, and re-layouts: 181 us -> 32 us
  Pallas kernels: 0 us -> 121 us
  waiting for transfers between devices: 161 us -> 70.1 us
  blocking collectives: 74.8 us -> 23.8 us
  matrix products: 57.3 us -> 11.1 us
  between operations: 14.9 us -> 0.99 us
    scatter-add x8 -> x0, other arithmetic: 180 us -> none  [the longest x4 144 us: apply_operator(): assembled = jnp.zeros((extended.shape[0], columns), jnp.float32).at[flat_...]
    psum x1 -> x0, waiting for transfers between devices: 139 us -> none  [local(): gram = lax.psum(self_gram(node_half), ('dx', 'dy', 'band')) / total_nodes]
    gather x8 -> x0, local copies, waits for them, and re-layouts: 121 us -> none  [the longest x4 100 us: apply_operator(): jnp.take(extended, flat_index, axis=0)]
    pallas_call x0 -> x11, Pallas kernels: none -> 121 us  [the longest x4 78.7 us: local(): call(kernel, [shape(wide * nodes, LANES), shape(wide * face_rows, LANES)]...]
    all_to_all x2 -> x1, blocking collectives: 74.8 us -> 23.8 us  [summed(): pieces = lax.all_to_all(pieces, axes, 0, 0, tiled=True)]
    dot_general x14 -> x4, matrix products: 57.3 us -> 11.1 us  [the longest x1 4.37 us: finish(): jnp.dot(exact, own, precision=lax.Precision.HIGHEST)]
    dot_general x4 -> x0, local copies, waits for them, and re-layouts: 26.3 us -> none  [apply_operator(): jnp.einsum('cpq,cqo->cpo', hamiltonian, cell_vals, preferred_element_type...]
    all_to_all x0 -> x1, waiting for transfers between devices: none -> 25.3 us  [summed(): lax.all_to_all(jnp.broadcast_to(piece, pieces.shape), axes, 0, 0, tiled=T...]
  transfers between devices with their start and end apart: 33 -> 35, of which waited for: 17 -> 18; matrix products, arithmetic and copies ran while one was open for 4% -> 4% of each run, Pallas kernels for 0% -> 8%
where the time goes in v1:
time: 330 us
  Pallas kernels  121 us (37%)
  waiting for transfers between devices  70.1 us (21%)
  starting transfers between devices  57 us (17%)
  local copies, waits for them, and re-layouts  32 us (10%)
  blocking collectives  23.8 us (7%)
  other arithmetic  13.5 us (4%)
  matrix products  11.1 us (3%)
    pallas_call x4, Pallas kernels, local(): call(kernel, [shape(wide * nodes, LANES), shape(wide * face_rows, LANES)]...  78.7 us
    ppermute x34, starting transfers between devices, passed_along(): return lax.ppermute(value, axis, pairs)  48.8 us
    ppermute x34, waiting for transfers between devices, passed_along(): return lax.ppermute(value, axis, pairs)  44.9 us
    all_to_all x1, waiting for transfers between devices, summed(): lax.all_to_all(jnp.broadcast_to(piece, pieces.shape), axes, 0, 0, tiled=T...  25.3 us
    all_to_all x1, blocking collectives, summed(): pieces = lax.all_to_all(pieces, axes, 0, 0, tiled=True)  23.8 us
    unnamed x37, local copies, waits for them, and re-layouts  22.5 us
    pallas_call x1, Pallas kernels, local(): call(index_kernel, [table, table], [SMEM], out_specs=[SMEM, SMEM], cost=p...  20 us
    pallas_call x3, Pallas kernels, local(): call(faces_kernel, [shape(wide * nodes, LANES), shape(wide * face_rows, L...  11.8 us
  transfers between devices with their start and end apart: 35, of which 18 were waited for; matrix products, arithmetic and copies ran while one was open for 4% of the time, Pallas kernels for 8%

profile of v1, /device:TPU:19, one launch (start us, length us, event | category | flops | bytes accessed | tf_op | source)
XLA Modules:
  0.0 329.6 jit_solution(6885283589689930773)
XLA Ops:
  0.7 1.9 copy-done.3
  2.6 2.0 shard_map.47
  4.6 1.7 copy-done.1
  6.3 1.3 collective-permute-start
  7.9 2.8 collective-permute-start.2
  10.6 20.0 %shard_map.46 = (s32[4096]{0:T(1024)S(1)}, s32[4096]{0:T(1024)S(1)}) custom-call(s32[6144]{0:T(1024)S(1)} %bitcast.26), custom_call_target="tpu_custom_call" | custom-call | flops 1000000000 | bytes 10000000 | tf_op jit(solution)/shard_map/pallas_call | solution.py:272
  32.1 2.8 copy-done
  34.9 1.9 copy-done.2
  36.7 19.6 %shard_map.48 = (f32[6144,128]{1,0:T(8,128)S(1)}, f32[2048,128]{1,0:T(8,128)S(1)}) custom-call(s32[6144]{0:T(1024)S(1)} %broadcast_multiply_fusion.refs_0_, s32[4096]{0:T(1024)S(1)} %get-tuple-element.25.refs_1_, s32[4096]{0:T(1024)S(1)} %get-tuple-element.26.refs_2_, s32[4096]{0:T(1024)S(1)} %broadcast_select_fusion.refs_3_, s32[1]{0:T(128)} %bitcast.1.refs_4_, ...), custom_call_target="tpu_custom_call" | custom-call | tf_op jit(solution)/shard_map/pallas_call | solution.py:289
  56.4 2.4 collective-permute-start.4
  58.9 1.7 collective-permute-start.6
  60.9 2.2 collective-permute-done.4.west
  63.1 1.9 collective-permute-done.5.east
  65.2 3.9 %shard_map.49 = (f32[6144,128]{1,0:T(8,128)S(1)}, bf16[2048,128]{1,0:T(8,128)(2,1)S(1)}) custom-call(s32[1024]{0:T(1024)S(1)} %bitcast.22, f32[6144,128]{1,0:T(8,128)S(1)} %get-tuple-element.29.partial, f32[512,128]{1,0:T(8,128)S(1)} %collective-permute-done.4.west, f32[512,128]{1,0:T(8,128)S(1)} %collective-permute-done.5.east, ...), custom_call_target="tpu_custom_call", output_to_operand_aliasing={{0}: (1, {})} | custom-call | tf_op jit(solution)/shard_map/pallas_call | solution.py:303
  69.2 3.9 %collective-permute-start.10 = (bf16[512,128]{1,0:T(8,128)(2,1)S(1)}, bf16[512,128]{1,0:T(8,128)(2,1)S(1)}, u32[]{:S(2)}, u32[]{:S(2)}) collective-permute-start(bf16[512,128]{1,0:T(8,128)(2,1)S(1)} %get-tuple-element.78), channel_id=1, source_target_pairs={{0,2},{2,4},{4,6},{6,8},{8,10},{10,12},{12,14},{14,0},{1,3},{3,5},... | collective-permute-start | bytes 393224 | tf_op jit(solution)/shard_map/ppermute | solution.py:228
  73.1 3.2 collective-permute-start.9
  76.3 1.4 collective-permute-done.11.refs_10_
  78.7 19.7 %shard_map.50 = (f32[6144,128]{1,0:T(8,128)S(1)}, f32[2048,128]{1,0:T(8,128)S(1)}) custom-call(s32[6144]{0:T(1024)S(1)} %broadcast_multiply_fusion.refs_0_, s32[4096]{0:T(1024)S(1)} %get-tuple-element.25.refs_1_, s32[4096]{0:T(1024)S(1)} %get-tuple-element.26.refs_2_, s32[4096]{0:T(1024)S(1)} %broadcast_select_fusion.refs_3_, s32[1]{0:T(128)} %bitcast.1.refs_4_, ...), custom_call_target="tpu_custom_call" | custom-call | tf_op jit(solution)/shard_map/pallas_call | solution.py:289
  98.5 3.6 %collective-permute-start.12 = (f32[512,128]{1,0:T(8,128)S(1)}, f32[512,128]{1,0:T(8,128)S(1)}, u32[]{:S(2)}, u32[]{:S(2)}) collective-permute-start(f32[512,128]{1,0:T(8,128)S(1)} %get-tuple-element.60), channel_id=1, source_target_pairs={{0,112},{16,0},{32,16},{48,32},{64,48},{80,64},{96,80},{112,96},{1... | collective-permute-start | bytes 786440 | tf_op jit(solution)/shard_map/ppermute | solution.py:228
  102.1 2.9 collective-permute-start.14
  105.7 4.0 %collective-permute-done.13.east = f32[512,128]{1,0:T(8,128)S(1)} collective-permute-done((f32[512,128]{1,0:T(8,128)S(1)}, f32[512,128]{1,0:T(8,128)S(1)}, u32[]{:S(2)}, u32[]{:S(2)}) %collective-permute-start.13) | collective-permute-done | bytes 262176 | tf_op jit(solution)/shard_map/ppermute | solution.py:228
  110.1 3.9 %shard_map.51 = (f32[6144,128]{1,0:T(8,128)S(1)}, bf16[2048,128]{1,0:T(8,128)(2,1)S(1)}) custom-call(s32[1024]{0:T(1024)S(1)} %bitcast.23, f32[6144,128]{1,0:T(8,128)S(1)} %get-tuple-element.33.partial, f32[512,128]{1,0:T(8,128)S(1)} %collective-permute-done.12.west, f32[512,128]{1,0:T(8,128)S(1)} %collective-permute-done.13.east, ...), custom_call_target="tpu_custom_call", output_to_operand_aliasing={{0}: (1, {})} | custom-call | tf_op jit(solution)/shard_map/pallas_call | solution.py:303
  114.0 2.4 collective-permute-start.16
  116.4 1.3 collective-permute-start.17
  117.8 4.8 %collective-permute-start.18 = (bf16[512,128]{1,0:T(8,128)(2,1)S(1)}, bf16[512,128]{1,0:T(8,128)(2,1)S(1)}, u32[]{:S(2)}, u32[]{:S(2)}) collective-permute-start(bf16[512,128]{1,0:T(8,128)(2,1)S(1)} %get-tuple-element.74), channel_id=1, source_target_pairs={{0,2},{2,4},{4,6},{6,8},{8,10},{10,12},{12,14},{14,0},{1,3},{3,5},... | collective-permute-start | bytes 393224 | tf_op jit(solution)/shard_map/ppermute | solution.py:228
  122.9 1.7 collective-permute-done.18.refs_9_
  124.5 2.4 collective-permute-done.19.refs_10_
  127.0 19.7 %shard_map.52 = (f32[6144,128]{1,0:T(8,128)S(1)}, f32[2048,128]{1,0:T(8,128)S(1)}) custom-call(s32[6144]{0:T(1024)S(1)} %broadcast_multiply_fusion.refs_0_, s32[4096]{0:T(1024)S(1)} %get-tuple-element.25.refs_1_, s32[4096]{0:T(1024)S(1)} %get-tuple-element.26.refs_2_, s32[4096]{0:T(1024)S(1)} %broadcast_select_fusion.refs_3_, s32[1]{0:T(128)} %bitcast.1.refs_4_, ...), custom_call_target="tpu_custom_call" | custom-call | tf_op jit(solution)/shard_map/pallas_call | solution.py:289
  146.8 3.8 %collective-permute-start.20 = (f32[512,128]{1,0:T(8,128)S(1)}, f32[512,128]{1,0:T(8,128)S(1)}, u32[]{:S(2)}, u32[]{:S(2)}) collective-permute-start(f32[512,128]{1,0:T(8,128)S(1)} %get-tuple-element.56), channel_id=1, source_target_pairs={{0,112},{16,0},{32,16},{48,32},{64,48},{80,64},{96,80},{112,96},{1... | collective-permute-start | bytes 786440 | tf_op jit(solution)/shard_map/ppermute | solution.py:228
  151.2 1.1 collective-permute-start.23
  152.4 3.6 %collective-permute-done.20.west = f32[512,128]{1,0:T(8,128)S(1)} collective-permute-done((f32[512,128]{1,0:T(8,128)S(1)}, f32[512,128]{1,0:T(8,128)S(1)}, u32[]{:S(2)}, u32[]{:S(2)}) %collective-permute-start.20) | collective-permute-done | bytes 262176 | tf_op jit(solution)/shard_map/ppermute | solution.py:228
  155.9 1.9 collective-permute-done.21.east
  157.9 3.9 %shard_map.53 = (f32[6144,128]{1,0:T(8,128)S(1)}, bf16[2048,128]{1,0:T(8,128)(2,1)S(1)}) custom-call(s32[1024]{0:T(1024)S(1)} %bitcast.24, f32[6144,128]{1,0:T(8,128)S(1)} %get-tuple-element.37.partial, f32[512,128]{1,0:T(8,128)S(1)} %collective-permute-done.20.west, f32[512,128]{1,0:T(8,128)S(1)} %collective-permute-done.21.east, ...), custom_call_target="tpu_custom_call", output_to_operand_aliasing={{0}: (1, {})} | custom-call | tf_op jit(solution)/shard_map/pallas_call | solution.py:303
  162.2 1.2 collective-permute-start.25
  163.4 3.2 collective-permute-start.26
  167.0 1.6 collective-permute-done.26.refs_9_
  168.6 2.7 collective-permute-done.27.refs_10_
  171.3 19.7 %shard_map.54 = (f32[6144,128]{1,0:T(8,128)S(1)}, f32[2048,128]{1,0:T(8,128)S(1)}) custom-call(s32[6144]{0:T(1024)S(1)} %broadcast_multiply_fusion.refs_0_, s32[4096]{0:T(1024)S(1)} %get-tuple-element.25.refs_1_, s32[4096]{0:T(1024)S(1)} %get-tuple-element.26.refs_2_, s32[4096]{0:T(1024)S(1)} %broadcast_select_fusion.refs_3_, s32[1]{0:T(128)} %bitcast.1.refs_4_, ...), custom_call_target="tpu_custom_call" | custom-call | tf_op jit(solution)/shard_map/pallas_call | solution.py:289
  191.0 1.7 copy-done.4
  192.8 3.8 %collective-permute-start.28 = (f32[512,128]{1,0:T(8,128)S(1)}, f32[512,128]{1,0:T(8,128)S(1)}, u32[]{:S(2)}, u32[]{:S(2)}) collective-permute-start(f32[512,128]{1,0:T(8,128)S(1)} %get-tuple-element.52), channel_id=1, source_target_pairs={{0,112},{16,0},{32,16},{48,32},{64,48},{80,64},{96,80},{112,96},{1... | collective-permute-start | bytes 786440 | tf_op jit(solution)/shard_map/ppermute | solution.py:228
  196.6 1.4 collective-permute-start.30
  198.3 2.8 collective-permute-done.28.west
  201.2 1.9 collective-permute-done.29.east
  205.2 1.9 copy-done.5
  210.0 2.8 shard_map.55
  212.8 1.1 copy-done.6
  213.9 1.3 constant_dynamic-slice_fusion
  215.6 2.6 select_convert_fusion.1
  218.1 14.9 %collective-permute-done.32 = bf16[1536,256]{1,0:T(8,128)(2,1)} collective-permute-done((bf16[1536,256]{1,0:T(8,128)(2,1)}, bf16[1536,256]{1,0:T(8,128)(2,1)}, u32[]{:S(2)}, u32[]{:S(2)}) %collective-permute-start.32) | collective-permute-done | bytes 786464 | tf_op jit(solution)/shard_map/ppermute | solution.py:228
  233.0 1.7 convolution_convert_fusion
  236.2 4.6 %reduce.3 = bf16[128,1536]{1,0:T(8,128)(2,1)} reduce(bf16[128,1,1536]{2,1,0:T(2,128)(2,1)} %convert_element_type.22, bf16[]{:T(256)} %broadcast.9), dimensions={1}, to_apply=%convert_element_type.22.reduce_sub_computation | reduce | bytes 786434 | tf_op jit(solution)/shard_map/convert_element_type | solution.py:327
  241.9 23.8 %all_to_all.12 = bf16[128,2,768]{2,1,0:T(2,128)(2,1)} all-to-all(bf16[128,2,768]{2,1,0:T(2,128)(2,1)S(1)} %reshape.105), channel_id=1, replica_groups=mesh['dx'=8,'dy'=8,'band'=2] {'dx','dy','band'}, dimensions={0} | all-to-all | bytes 786432 | tf_op jit(solution)/shard_map/all_to_all | solution.py:328
  265.7 3.5 %reshape.106 = bf16[128,1,1536]{2,1,0:T(2,128)(2,1)} reshape(bf16[128,2,768]{2,1,0:T(2,128)(2,1)} %all_to_all.12) | data formatting | bytes 786432
  269.2 1.9 convert_reduce_fusion
  271.1 1.3 broadcast_in_dim.28
  272.4 8.2 %all-to-all-start.1 = ((f32[128,1,1536]{2,1,0:T(1,128)}), f32[128,1,1536]{2,1,0:T(1,128)}, u32[]{:S(2)}, u32[]{:S(2)}) async-start(f32[128,1,1536]{2,1,0:T(1,128)} %broadcast_in_dim.28), calls=%async_computation.1 | async-start | bytes 1572864 | tf_op jit(solution)/shard_map/all_to_all | solution.py:330
  281.0 25.3 %all-to-all-done.1 = f32[128,1,1536]{2,1,0:T(1,128)} async-done(((f32[128,1,1536]{2,1,0:T(1,128)}), f32[128,1,1536]{2,1,0:T(1,128)}, u32[]{:S(2)}, u32[]{:S(2)}) %all-to-all-start.1) | async-done | bytes 786464 | tf_op jit(solution)/shard_map/all_to_all | solution.py:330
  306.3 4.3 %multiply_reduce_fusion = f32[128,1536]{1,0:T(8,128)} fusion(f32[128,1,1536]{2,1,0:T(1,128)} %all-to-all-done.1), kind=kLoop, calls=%fused_computation.12 | loop fusion | flops 196608 | bytes 1572864 | tf_op jit(solution)/shard_map/div | solution.py:349
  310.6 2.2 div.10
  312.8 2.0 fusion.17
  315.7 1.3 maximum_maximum_fusion.gram
  317.0 5.8 %shard_map.56 = f32[512,512]{1,0:T(8,128)S(1)} custom-call(f32[512,512]{1,0:T(8,128)S(1)} %maximum_maximum_fusion.gram), custom_call_target="tpu_custom_call" | custom-call | tf_op jit(solution)/shard_map/pallas_call | solution.py:354
  322.7 2.5 fusion.1
  325.2 4.4 %fusion = f32[1,1,3072,256]{3,2,1,0:T(8,128)} fusion(f32[3072,256]{1,0:T(8,128)S(1)} %fusion.1, f32[3072,256]{1,0:T(8,128)S(1)} %get-tuple-element.43, f32[512,512]{1,0:T(8,128)S(1)} %shard_map.56, s32[]{:T(128)S(6)} %select_n.69), kind=kOutput, calls=%fused_computation.1 | convolution fusion | flops 2416705536 | bytes 9699332 | tf_op jit(solution)/shard_map/dot_general | solution.py:358
  (84 shorter events, 15.9 us)
Async XLA Ops:
  0.7 1.9 copy-start.3
  2.6 8.0 %copy-start.13 = (s32[1,1,12,512]{3,1,2,0:T(1,128)S(1)}, s32[1,1,12,512]{3,1,2,0:T(1,128)}, u32[]{:S(2)}) copy-start(s32[1,1,12,512]{3,1,2,0:T(1,128)} %param.6) | copy-start | bytes 73732
  4.6 1.7 copy-start.1
  6.3 25.7 %collective-permute-start = (bf16[512,128]{1,0:T(8,128)(2,1)S(1)}, bf16[512,128]{1,0:T(8,128)(2,1)S(1)}, u32[]{:S(2)}, u32[]{:S(2)}) collective-permute-start(bf16[512,128]{1,0:T(8,128)(2,1)S(1)} %get-tuple-element.84), channel_id=1, source_target_pairs={{0,16},{16,32},{32,48},{48,64},{64,80},{80,96},{96,112},{112,0},{1... | collective-permute-start | bytes 393224 | tf_op jit(solution)/shard_map/ppermute | solution.py:228
  7.6 24.4 %collective-permute-start.1 = (bf16[512,128]{1,0:T(8,128)(2,1)S(1)}, bf16[512,128]{1,0:T(8,128)(2,1)S(1)}, u32[]{:S(2)}, u32[]{:S(2)}) collective-permute-start(bf16[512,128]{1,0:T(8,128)(2,1)S(1)} %get-tuple-element.83), channel_id=1, source_target_pairs={{0,112},{16,0},{32,16},{48,32},{64,48},{80,64},{96,80},{112,96},{1... | collective-permute-start | bytes 393224 | tf_op jit(solution)/shard_map/ppermute | solution.py:228
  7.9 24.2 %collective-permute-start.2 = (bf16[512,128]{1,0:T(8,128)(2,1)S(1)}, bf16[512,128]{1,0:T(8,128)(2,1)S(1)}, u32[]{:S(2)}, u32[]{:S(2)}) collective-permute-start(bf16[512,128]{1,0:T(8,128)(2,1)S(1)} %get-tuple-element.82), channel_id=1, source_target_pairs={{0,2},{2,4},{4,6},{6,8},{8,10},{10,12},{12,14},{14,0},{1,3},{3,5},... | collective-permute-start | bytes 393224 | tf_op jit(solution)/shard_map/ppermute | solution.py:228
  10.6 21.4 %collective-permute-start.3 = (bf16[512,128]{1,0:T(8,128)(2,1)S(1)}, bf16[512,128]{1,0:T(8,128)(2,1)S(1)}, u32[]{:S(2)}, u32[]{:S(2)}) collective-permute-start(bf16[512,128]{1,0:T(8,128)(2,1)S(1)} %get-tuple-element.81), channel_id=1, source_target_pairs={{0,14},{2,0},{4,2},{6,4},{8,6},{10,8},{12,10},{14,12},{1,15},{3,1}... | collective-permute-start | bytes 393224 | tf_op jit(solution)/shard_map/ppermute | solution.py:228
  10.6 68.0 %slice-start = ((s8[6291456]{0:T(1024)(128)(4,1)}), s8[2097152]{0:T(1024)(128)(4,1)S(1)}, s32[]{:S(2)}) async-start(s8[6291456]{0:T(1024)(128)(4,1)} %bitcast.15), calls=%async_computation.2 | async-start | bytes 4194304
  32.1 2.8 copy-start
  34.8 1.9 copy-start.2
  36.7 41.9 %slice-start.1 = ((s8[6291456]{0:T(1024)(128)(4,1)}), s8[4194304]{0:T(1024)(128)(4,1)S(1)}, s32[]{:S(2)}) async-start(s8[6291456]{0:T(1024)(128)(4,1)} %bitcast.15), calls=%async_computation.3 | async-start | bytes 8388608
  56.4 6.7 %collective-permute-start.4 = (f32[512,128]{1,0:T(8,128)S(1)}, f32[512,128]{1,0:T(8,128)S(1)}, u32[]{:S(2)}, u32[]{:S(2)}) collective-permute-start(f32[512,128]{1,0:T(8,128)S(1)} %get-tuple-element.64), channel_id=1, source_target_pairs={{0,112},{16,0},{32,16},{48,32},{64,48},{80,64},{96,80},{112,96},{1... | collective-permute-start | bytes 786440 | tf_op jit(solution)/shard_map/ppermute | solution.py:228
  58.9 6.2 %collective-permute-start.5 = (f32[512,128]{1,0:T(8,128)S(1)}, f32[512,128]{1,0:T(8,128)S(1)}, u32[]{:S(2)}, u32[]{:S(2)}) collective-permute-start(f32[512,128]{1,0:T(8,128)S(1)} %get-tuple-element.63), channel_id=1, source_target_pairs={{0,16},{16,32},{32,48},{48,64},{64,80},{80,96},{96,112},{112,0},{1... | collective-permute-start | bytes 786440 | tf_op jit(solution)/shard_map/ppermute | solution.py:228
  58.9 6.4 %collective-permute-start.6 = (f32[512,128]{1,0:T(8,128)S(1)}, f32[512,128]{1,0:T(8,128)S(1)}, u32[]{:S(2)}, u32[]{:S(2)}) collective-permute-start(f32[512,128]{1,0:T(8,128)S(1)} %get-tuple-element.62), channel_id=1, source_target_pairs={{0,14},{2,0},{4,2},{6,4},{8,6},{10,8},{12,10},{14,12},{1,15},{3,1}... | collective-permute-start | bytes 786440 | tf_op jit(solution)/shard_map/ppermute | solution.py:228
  60.6 4.7 %collective-permute-start.7 = (f32[512,128]{1,0:T(8,128)S(1)}, f32[512,128]{1,0:T(8,128)S(1)}, u32[]{:S(2)}, u32[]{:S(2)}) collective-permute-start(f32[512,128]{1,0:T(8,128)S(1)} %get-tuple-element.61), channel_id=1, source_target_pairs={{0,2},{2,4},{4,6},{6,8},{8,10},{10,12},{12,14},{14,0},{1,3},{3,5},... | collective-permute-start | bytes 786440 | tf_op jit(solution)/shard_map/ppermute | solution.py:228
  69.2 7.1 %collective-permute-start.10 = (bf16[512,128]{1,0:T(8,128)(2,1)S(1)}, bf16[512,128]{1,0:T(8,128)(2,1)S(1)}, u32[]{:S(2)}, u32[]{:S(2)}) collective-permute-start(bf16[512,128]{1,0:T(8,128)(2,1)S(1)} %get-tuple-element.78), channel_id=1, source_target_pairs={{0,2},{2,4},{4,6},{6,8},{8,10},{10,12},{12,14},{14,0},{1,3},{3,5},... | collective-permute-start | bytes 393224 | tf_op jit(solution)/shard_map/ppermute | solution.py:228
  73.1 4.6 %collective-permute-start.11 = (bf16[512,128]{1,0:T(8,128)(2,1)S(1)}, bf16[512,128]{1,0:T(8,128)(2,1)S(1)}, u32[]{:S(2)}, u32[]{:S(2)}) collective-permute-start(bf16[512,128]{1,0:T(8,128)(2,1)S(1)} %get-tuple-element.77), channel_id=1, source_target_pairs={{0,14},{2,0},{4,2},{6,4},{8,6},{10,8},{12,10},{14,12},{1,15},{3,1}... | collective-permute-start | bytes 393224 | tf_op jit(solution)/shard_map/ppermute | solution.py:228
  73.1 5.6 %collective-permute-start.8 = (bf16[512,128]{1,0:T(8,128)(2,1)S(1)}, bf16[512,128]{1,0:T(8,128)(2,1)S(1)}, u32[]{:S(2)}, u32[]{:S(2)}) collective-permute-start(bf16[512,128]{1,0:T(8,128)(2,1)S(1)} %get-tuple-element.80), channel_id=1, source_target_pairs={{0,16},{16,32},{32,48},{48,64},{64,80},{80,96},{96,112},{112,0},{1... | collective-permute-start | bytes 393224 | tf_op jit(solution)/shard_map/ppermute | solution.py:228
  73.1 5.6 %collective-permute-start.9 = (bf16[512,128]{1,0:T(8,128)(2,1)S(1)}, bf16[512,128]{1,0:T(8,128)(2,1)S(1)}, u32[]{:S(2)}, u32[]{:S(2)}) collective-permute-start(bf16[512,128]{1,0:T(8,128)(2,1)S(1)} %get-tuple-element.79), channel_id=1, source_target_pairs={{0,112},{16,0},{32,16},{48,32},{64,48},{80,64},{96,80},{112,96},{1... | collective-permute-start | bytes 393224 | tf_op jit(solution)/shard_map/ppermute | solution.py:228
  98.5 7.2 %collective-permute-start.12 = (f32[512,128]{1,0:T(8,128)S(1)}, f32[512,128]{1,0:T(8,128)S(1)}, u32[]{:S(2)}, u32[]{:S(2)}) collective-permute-start(f32[512,128]{1,0:T(8,128)S(1)} %get-tuple-element.60), channel_id=1, source_target_pairs={{0,112},{16,0},{32,16},{48,32},{64,48},{80,64},{96,80},{112,96},{1... | collective-permute-start | bytes 786440 | tf_op jit(solution)/shard_map/ppermute | solution.py:228
  102.1 7.6 %collective-permute-start.13 = (f32[512,128]{1,0:T(8,128)S(1)}, f32[512,128]{1,0:T(8,128)S(1)}, u32[]{:S(2)}, u32[]{:S(2)}) collective-permute-start(f32[512,128]{1,0:T(8,128)S(1)} %get-tuple-element.59), channel_id=1, source_target_pairs={{0,16},{16,32},{32,48},{48,64},{64,80},{80,96},{96,112},{112,0},{1... | collective-permute-start | bytes 786440 | tf_op jit(solution)/shard_map/ppermute | solution.py:228
  102.1 7.9 %collective-permute-start.14 = (f32[512,128]{1,0:T(8,128)S(1)}, f32[512,128]{1,0:T(8,128)S(1)}, u32[]{:S(2)}, u32[]{:S(2)}) collective-permute-start(f32[512,128]{1,0:T(8,128)S(1)} %get-tuple-element.58), channel_id=1, source_target_pairs={{0,14},{2,0},{4,2},{6,4},{8,6},{10,8},{12,10},{14,12},{1,15},{3,1}... | collective-permute-start | bytes 786440 | tf_op jit(solution)/shard_map/ppermute | solution.py:228
  105.0 5.1 %collective-permute-start.15 = (f32[512,128]{1,0:T(8,128)S(1)}, f32[512,128]{1,0:T(8,128)S(1)}, u32[]{:S(2)}, u32[]{:S(2)}) collective-permute-start(f32[512,128]{1,0:T(8,128)S(1)} %get-tuple-element.57), channel_id=1, source_target_pairs={{0,2},{2,4},{4,6},{6,8},{8,10},{10,12},{12,14},{14,0},{1,3},{3,5},... | collective-permute-start | bytes 786440 | tf_op jit(solution)/shard_map/ppermute | solution.py:228
  114.0 8.5 %collective-permute-start.16 = (bf16[512,128]{1,0:T(8,128)(2,1)S(1)}, bf16[512,128]{1,0:T(8,128)(2,1)S(1)}, u32[]{:S(2)}, u32[]{:S(2)}) collective-permute-start(bf16[512,128]{1,0:T(8,128)(2,1)S(1)} %get-tuple-element.76), channel_id=1, source_target_pairs={{0,16},{16,32},{32,48},{48,64},{64,80},{80,96},{96,112},{112,0},{1... | collective-permute-start | bytes 393224 | tf_op jit(solution)/shard_map/ppermute | solution.py:228
  116.4 6.4 %collective-permute-start.17 = (bf16[512,128]{1,0:T(8,128)(2,1)S(1)}, bf16[512,128]{1,0:T(8,128)(2,1)S(1)}, u32[]{:S(2)}, u32[]{:S(2)}) collective-permute-start(bf16[512,128]{1,0:T(8,128)(2,1)S(1)} %get-tuple-element.75), channel_id=1, source_target_pairs={{0,112},{16,0},{32,16},{48,32},{64,48},{80,64},{96,80},{112,96},{1... | collective-permute-start | bytes 393224 | tf_op jit(solution)/shard_map/ppermute | solution.py:228
  117.8 6.8 %collective-permute-start.18 = (bf16[512,128]{1,0:T(8,128)(2,1)S(1)}, bf16[512,128]{1,0:T(8,128)(2,1)S(1)}, u32[]{:S(2)}, u32[]{:S(2)}) collective-permute-start(bf16[512,128]{1,0:T(8,128)(2,1)S(1)} %get-tuple-element.74), channel_id=1, source_target_pairs={{0,2},{2,4},{4,6},{6,8},{8,10},{10,12},{12,14},{14,0},{1,3},{3,5},... | collective-permute-start | bytes 393224 | tf_op jit(solution)/shard_map/ppermute | solution.py:228
  122.6 4.4 %collective-permute-start.19 = (bf16[512,128]{1,0:T(8,128)(2,1)S(1)}, bf16[512,128]{1,0:T(8,128)(2,1)S(1)}, u32[]{:S(2)}, u32[]{:S(2)}) collective-permute-start(bf16[512,128]{1,0:T(8,128)(2,1)S(1)} %get-tuple-element.73), channel_id=1, source_target_pairs={{0,14},{2,0},{4,2},{6,4},{8,6},{10,8},{12,10},{14,12},{1,15},{3,1}... | collective-permute-start | bytes 393224 | tf_op jit(solution)/shard_map/ppermute | solution.py:228
  146.8 9.2 %collective-permute-start.20 = (f32[512,128]{1,0:T(8,128)S(1)}, f32[512,128]{1,0:T(8,128)S(1)}, u32[]{:S(2)}, u32[]{:S(2)}) collective-permute-start(f32[512,128]{1,0:T(8,128)S(1)} %get-tuple-element.56), channel_id=1, source_target_pairs={{0,112},{16,0},{32,16},{48,32},{64,48},{80,64},{96,80},{112,96},{1... | collective-permute-start | bytes 786440 | tf_op jit(solution)/shard_map/ppermute | solution.py:228
  150.6 7.2 %collective-permute-start.21 = (f32[512,128]{1,0:T(8,128)S(1)}, f32[512,128]{1,0:T(8,128)S(1)}, u32[]{:S(2)}, u32[]{:S(2)}) collective-permute-start(f32[512,128]{1,0:T(8,128)S(1)} %get-tuple-element.55), channel_id=1, source_target_pairs={{0,16},{16,32},{32,48},{48,64},{64,80},{80,96},{96,112},{112,0},{1... | collective-permute-start | bytes 786440 | tf_op jit(solution)/shard_map/ppermute | solution.py:228
  150.6 7.2 %collective-permute-start.22 = (f32[512,128]{1,0:T(8,128)S(1)}, f32[512,128]{1,0:T(8,128)S(1)}, u32[]{:S(2)}, u32[]{:S(2)}) collective-permute-start(f32[512,128]{1,0:T(8,128)S(1)} %get-tuple-element.54), channel_id=1, source_target_pairs={{0,14},{2,0},{4,2},{6,4},{8,6},{10,8},{12,10},{14,12},{1,15},{3,1}... | collective-permute-start | bytes 786440 | tf_op jit(solution)/shard_map/ppermute | solution.py:228
  151.2 6.6 %collective-permute-start.23 = (f32[512,128]{1,0:T(8,128)S(1)}, f32[512,128]{1,0:T(8,128)S(1)}, u32[]{:S(2)}, u32[]{:S(2)}) collective-permute-start(f32[512,128]{1,0:T(8,128)S(1)} %get-tuple-element.53), channel_id=1, source_target_pairs={{0,2},{2,4},{4,6},{6,8},{8,10},{10,12},{12,14},{14,0},{1,3},{3,5},... | collective-permute-start | bytes 786440 | tf_op jit(solution)/shard_map/ppermute | solution.py:228
  161.8 5.2 %collective-permute-start.24 = (bf16[512,128]{1,0:T(8,128)(2,1)S(1)}, bf16[512,128]{1,0:T(8,128)(2,1)S(1)}, u32[]{:S(2)}, u32[]{:S(2)}) collective-permute-start(bf16[512,128]{1,0:T(8,128)(2,1)S(1)} %get-tuple-element.72), channel_id=1, source_target_pairs={{0,16},{16,32},{32,48},{48,64},{64,80},{80,96},{96,112},{112,0},{1... | collective-permute-start | bytes 393224 | tf_op jit(solution)/shard_map/ppermute | solution.py:228
  162.2 4.8 %collective-permute-start.25 = (bf16[512,128]{1,0:T(8,128)(2,1)S(1)}, bf16[512,128]{1,0:T(8,128)(2,1)S(1)}, u32[]{:S(2)}, u32[]{:S(2)}) collective-permute-start(bf16[512,128]{1,0:T(8,128)(2,1)S(1)} %get-tuple-element.71), channel_id=1, source_target_pairs={{0,112},{16,0},{32,16},{48,32},{64,48},{80,64},{96,80},{112,96},{1... | collective-permute-start | bytes 393224 | tf_op jit(solution)/shard_map/ppermute | solution.py:228
  163.4 5.2 %collective-permute-start.26 = (bf16[512,128]{1,0:T(8,128)(2,1)S(1)}, bf16[512,128]{1,0:T(8,128)(2,1)S(1)}, u32[]{:S(2)}, u32[]{:S(2)}) collective-permute-start(bf16[512,128]{1,0:T(8,128)(2,1)S(1)} %get-tuple-element.70), channel_id=1, source_target_pairs={{0,2},{2,4},{4,6},{6,8},{8,10},{10,12},{12,14},{14,0},{1,3},{3,5},... | collective-permute-start | bytes 393224 | tf_op jit(solution)/shard_map/ppermute | solution.py:228
  166.6 4.7 %collective-permute-start.27 = (bf16[512,128]{1,0:T(8,128)(2,1)S(1)}, bf16[512,128]{1,0:T(8,128)(2,1)S(1)}, u32[]{:S(2)}, u32[]{:S(2)}) collective-permute-start(bf16[512,128]{1,0:T(8,128)(2,1)S(1)} %get-tuple-element.69), channel_id=1, source_target_pairs={{0,14},{2,0},{4,2},{6,4},{8,6},{10,8},{12,10},{14,12},{1,15},{3,1}... | collective-permute-start | bytes 393224 | tf_op jit(solution)/shard_map/ppermute | solution.py:228
  191.0 1.7 copy-start.4
  192.8 8.4 %collective-permute-start.28 = (f32[512,128]{1,0:T(8,128)S(1)}, f32[512,128]{1,0:T(8,128)S(1)}, u32[]{:S(2)}, u32[]{:S(2)}) collective-permute-start(f32[512,128]{1,0:T(8,128)S(1)} %get-tuple-element.52), channel_id=1, source_target_pairs={{0,112},{16,0},{32,16},{48,32},{64,48},{80,64},{96,80},{112,96},{1... | collective-permute-start | bytes 786440 | tf_op jit(solution)/shard_map/ppermute | solution.py:228
  196.6 6.5 %collective-permute-start.29 = (f32[512,128]{1,0:T(8,128)S(1)}, f32[512,128]{1,0:T(8,128)S(1)}, u32[]{:S(2)}, u32[]{:S(2)}) collective-permute-start(f32[512,128]{1,0:T(8,128)S(1)} %get-tuple-element.51), channel_id=1, source_target_pairs={{0,16},{16,32},{32,48},{48,64},{64,80},{80,96},{96,112},{112,0},{1... | collective-permute-start | bytes 786440 | tf_op jit(solution)/shard_map/ppermute | solution.py:228
  196.6 7.2 %collective-permute-start.30 = (f32[512,128]{1,0:T(8,128)S(1)}, f32[512,128]{1,0:T(8,128)S(1)}, u32[]{:S(2)}, u32[]{:S(2)}) collective-permute-start(f32[512,128]{1,0:T(8,128)S(1)} %get-tuple-element.50), channel_id=1, source_target_pairs={{0,14},{2,0},{4,2},{6,4},{8,6},{10,8},{12,10},{14,12},{1,15},{3,1}... | collective-permute-start | bytes 786440 | tf_op jit(solution)/shard_map/ppermute | solution.py:228
  198.0 6.6 %collective-permute-start.31 = (f32[512,128]{1,0:T(8,128)S(1)}, f32[512,128]{1,0:T(8,128)S(1)}, u32[]{:S(2)}, u32[]{:S(2)}) collective-permute-start(f32[512,128]{1,0:T(8,128)S(1)} %get-tuple-element.49), channel_id=1, source_target_pairs={{0,2},{2,4},{4,6},{6,8},{8,10},{10,12},{12,14},{14,0},{1,3},{3,5},... | collective-permute-start | bytes 786440 | tf_op jit(solution)/shard_map/ppermute | solution.py:228
  203.1 0.7 copy-start.7
  203.8 0.7 copy-start.9
  204.5 0.7 copy-start.11
  205.2 1.9 copy-start.5
  207.1 0.9 copy-start.8
  208.1 0.9 copy-start.10
  209.0 0.9 copy-start.12
  212.8 1.1 copy-start.6
  215.2 17.8 %collective-permute-start.32 = (bf16[1536,256]{1,0:T(8,128)(2,1)}, bf16[1536,256]{1,0:T(8,128)(2,1)}, u32[]{:S(2)}, u32[]{:S(2)}) collective-permute-start(bf16[1536,256]{1,0:T(8,128)(2,1)} %get-tuple-element.47), channel_id=1, source_target_pairs={{0,1},{1,0},{2,3},{3,2},{4,5},{5,4},{6,7},{7,6},{8,9},{9,8},{10,11... | collective-permute-start | bytes 2359304 | tf_op jit(solution)/shard_map/ppermute | solution.py:228
  215.6 17.4 %copy-start.14 = (bf16[1536,256]{1,0:T(8,128)(2,1)S(1)}, bf16[1536,256]{1,0:T(8,128)(2,1)}, u32[]{:S(2)}) copy-start(bf16[1536,256]{1,0:T(8,128)(2,1)} %get-tuple-element.48) | copy-start | bytes 2359300
  272.4 33.9 %all-to-all-start.1 = ((f32[128,1,1536]{2,1,0:T(1,128)}), f32[128,1,1536]{2,1,0:T(1,128)}, u32[]{:S(2)}, u32[]{:S(2)}) async-start(f32[128,1,1536]{2,1,0:T(1,128)} %broadcast_in_dim.28), calls=%async_computation.1 | async-start | bytes 1572864 | tf_op jit(solution)/shard_map/all_to_all | solution.py:330
  280.6 42.2 %collective-permute-start.33 = (bf16[1536,256]{1,0:T(8,128)(2,1)}, bf16[1536,256]{1,0:T(8,128)(2,1)}, u32[]{:S(2)}, u32[]{:S(2)}) collective-permute-start(bf16[1536,256]{1,0:T(8,128)(2,1)} %get-tuple-element.48), channel_id=1, source_target_pairs={{0,1},{1,0},{2,3},{3,2},{4,5},{5,4},{6,7},{7,6},{8,9},{9,8},{10,11... | collective-permute-start | bytes 2359304 | tf_op jit(solution)/shard_map/ppermute | solution.py:228

commit v2 on v1

v2 whole, which is shorter than its diff:
```python
import jax
import jax.numpy as jnp
from jax import lax
from jax.experimental import pallas as pl
from jax.experimental.pallas import tpu as pltpu
from jax.sharding import PartitionSpec as P

NS_STEPS = 3
LANES = 128
UNROLL = 64
DISTINCT = 32


VMEM = pl.BlockSpec(memory_space=pltpu.VMEM)
SMEM = pl.BlockSpec(memory_space=pltpu.SMEM)


def limit(mib):
    return pltpu.CompilerParams(vmem_limit_bytes=mib << 20)


def pair(start):
    return pl.ds(pl.multiple_of(start, 2), 2)


def gather_rows(index, base, source, target, count):
    def step(number, carry):
        first = number * UNROLL
        for lane in range(UNROLL):
            row = index[base + first + lane]
            target[pair(2 * first + 2 * lane), :] = source[pair(row), :]
        return carry

    lax.fori_loop(0, count // UNROLL, step, 0)


def table_kernel(connection, one, two, extra):
    slots = connection.shape[1]
    high, low = one.shape
    chunk = 512

    def step(number, total):
        begin = pl.multiple_of(number * chunk, chunk)
        row = connection[:, pl.ds(begin, chunk)]
        slot = begin + lax.broadcasted_iota(jnp.int32, (1, chunk), 1)
        tens = (slot >> 7).astype(jnp.float32)
        units = (slot & 127).astype(jnp.float32)

        def weighted(value, size):
            hit = lax.broadcasted_iota(jnp.int32, (size, chunk), 0) == value
            return jnp.concatenate(
                [jnp.where(hit, jnp.broadcast_to(weight, hit.shape), 0.0) for weight in (jnp.ones_like(tens), tens, units)],
                axis=0,
            ).astype(jnp.bfloat16)

        return total + lax.dot_general(
            weighted(row >> 7, high), weighted(row & 127, low), (((1,), (1,)), ((), ())),
            preferred_element_type=jnp.float32,
        )

    total = lax.fori_loop(0, slots // chunk, step, jnp.zeros((3 * high, 3 * low), jnp.float32))

    def block(left, right):
        return total[left * high:(left + 1) * high, right * low:(right + 1) * low]

    count = block(0, 0)

    def whole(value):
        return value.astype(jnp.int32)

    summed_slots = 128 * whole(block(0, 1)) + whole(block(0, 2))
    squares = 16384 * whole(block(1, 1)) + 256 * whole(block(1, 2)) + whole(block(2, 2))
    apart = whole(jnp.sqrt(jnp.maximum(2 * squares - summed_slots * summed_slots, 0).astype(jnp.float32)) + 0.5)
    single = count < 1.5
    one[...] = jnp.where(single, 2 * summed_slots, summed_slots - apart)
    two[...] = jnp.where(single, 2 * slots, summed_slots + apart)
    extra[0] = jnp.where(jnp.max(count) > 2.5, 1, 0).astype(jnp.int32)


def start_kernel(faces, field, current, face_vals, held):
    nodes = field.shape[0]
    chunk = 256

    def step(number, carry):
        block = field[pl.ds(pl.multiple_of(number * chunk, chunk), chunk), :]
        begin = number * 2 * chunk
        current[pl.ds(begin, chunk, stride=2), :] = block[:, :LANES]
        current[pl.ds(begin + 1, chunk, stride=2), :] = block[:, LANES:]
        return carry

    lax.fori_loop(0, nodes // chunk, step, 0)
    gather_rows(faces, 0, current, held, faces.shape[0])
    face_vals[...] = held[...].astype(jnp.bfloat16)


def combine(connection, one, two, extra, products, target, begin, rows):
    @pl.when(extra[0] == 0)
    def _():
        def step(number, carry):
            base = number * UNROLL
            for lane in range(UNROLL):
                left = one[begin + base + lane]
                right = two[begin + base + lane]
                target[pair(2 * base + 2 * lane), :] = products[pair(left), :] + products[pair(right), :]
            return carry

        lax.fori_loop(0, rows // UNROLL, step, 0)

    @pl.when(extra[0] != 0)
    def _():
        def clear(number, carry):
            target[pl.ds(pl.multiple_of(number * 128, 128), 128), :] = jnp.zeros((128, LANES), jnp.float32)
            return carry

        lax.fori_loop(0, 2 * rows // 128, clear, 0)

        def add(slot, carry):
            row = connection[slot] - 2 * begin

            @pl.when(jnp.logical_and(row >= 0, row < 2 * rows))
            def _():
                target[pair(row), :] = target[pair(row), :] + products[pair(2 * slot), :]

            return carry

        lax.fori_loop(0, connection.shape[0], add, 0)


def cells_kernel(alpha, connection, one, two, extra, current, west, east, south, north, hamiltonian,
                 products, ghosts, extended, cell_in):
    owned = current.shape[0]
    face = west.shape[0]
    cells, points, _ = hamiltonian.shape
    chunk = 512

    def fill(number, carry):
        rows = pl.ds(pl.multiple_of(number * chunk, chunk), chunk)
        extended[rows, :] = current[rows, :]
        return carry

    lax.fori_loop(0, owned // chunk, fill, 0)
    for number, block in enumerate((west, east, south, north)):
        extended[pl.ds(owned + number * face, face), :] = block[...].astype(jnp.float32)
    products[pl.ds(2 * cells * points, 8), :] = jnp.zeros((8, LANES), jnp.float32)

    def cell(number, carry):
        gather_rows(connection, number * points, extended, cell_in, points)
        left = cell_in[pl.ds(0, points, stride=2), :].astype(jnp.bfloat16)
        right = cell_in[pl.ds(1, points, stride=2), :].astype(jnp.bfloat16)
        product = jnp.dot(
            hamiltonian[number],
            jnp.concatenate([left, right], axis=1),
            preferred_element_type=jnp.float32,
        )
        begin = number * 2 * points
        products[pl.ds(begin, points, stride=2), :] = product[:, :LANES]
        products[pl.ds(begin + 1, points, stride=2), :] = product[:, LANES:]
        return carry

    lax.fori_loop(0, cells, cell, 0)
    combine(connection, one, two, extra, products, ghosts, owned // 2, 2 * face)
    if alpha != 1.0:
        ghosts[...] = alpha * ghosts[...]


def owned_kernel(scales, connection, one, two, extra, products, current, before, partial):
    alpha, beta, gamma = scales
    owned = partial.shape[0]
    combine(connection, one, two, extra, products, partial, 0, owned // 2)
    chunk = 512

    def finish(number, carry):
        rows = pl.ds(pl.multiple_of(number * chunk, chunk), chunk)
        value = alpha * partial[rows, :] - beta * current[rows, :]
        if gamma:
            value = value - gamma * before[rows, :]
        partial[rows, :] = value
        return carry

    lax.fori_loop(0, owned // chunk, finish, 0)


def add_returned(faces, returned, target):
    count = faces.shape[0] // len(returned)
    for number, block in enumerate(returned):

        def step(turn, carry):
            base = turn * DISTINCT
            rows = [faces[number * count + base + lane] for lane in range(DISTINCT)]
            sums = [
                target[pair(rows[lane]), :] + block[pair(2 * base + 2 * lane), :] for lane in range(DISTINCT)
            ]
            for lane in range(DISTINCT):
                target[pair(rows[lane]), :] = sums[lane]
            return carry

        lax.fori_loop(0, count // DISTINCT, step, 0)


def faces_kernel(faces, partial, west, east, south, north, current, face_vals, held):
    add_returned(faces, (west, east, south, north), current)
    gather_rows(faces, 0, current, held, faces.shape[0])
    face_vals[...] = held[...].astype(jnp.bfloat16)


def last_kernel(band, faces, partial, west, east, south, north, exact, mine, theirs, work):
    add_returned(faces, (west, east, south, north), work)
    half = mine.shape[0]
    chunk = 256

    for start, rounded in ((band[0] * half, mine), ((1 - band[0]) * half, theirs)):

        def step(number, carry):
            inner = pl.multiple_of(number * chunk, chunk)
            outer = pl.multiple_of(start + inner, chunk)
            block = jnp.concatenate(
                [work[pl.ds(2 * outer, chunk, stride=2), :], work[pl.ds(2 * outer + 1, chunk, stride=2), :]],
                axis=1,
            )
            exact[pl.ds(outer, chunk), :] = block
            rounded[pl.ds(inner, chunk), :] = block.astype(jnp.bfloat16)
            return carry

        lax.fori_loop(0, half // chunk, step, 0)


def halves(value):
    high = value.astype(jnp.bfloat16)
    return high, (value - high.astype(jnp.float32)).astype(jnp.bfloat16)


def product3(left, right):
    def dot(a, b):
        return jnp.dot(a, b, preferred_element_type=jnp.float32)

    (lh, ll), (rh, rl) = halves(left), halves(right)
    return dot(lh, rh) + (dot(lh, rl) + dot(ll, rh))


def sum_kernel(scale, pieces, sums):
    total = jnp.sum(pieces[...].astype(jnp.float32), axis=0) * scale
    sums[...] = jnp.broadcast_to(total.astype(jnp.bfloat16)[None], sums.shape)


def rotate_kernel(band, blocks, exact, near, far, rotated, factor, work, sems):
    size = exact.shape[1]

    def square(which, part):
        begin = part * 2 * size
        return jnp.concatenate(
            [blocks[which, begin:begin + size, :], blocks[which, begin + size:begin + 2 * size, :]], axis=1
        ).astype(jnp.float32)

    me = band[0]
    cross = square(me, 1) + square(1 - me, 1).T
    value = jnp.concatenate(
        [
            jnp.concatenate([square(me, 0), cross], axis=1),
            jnp.concatenate([cross.T, square(1 - me, 0)], axis=1),
        ],
        axis=0,
    )
    scale = jnp.sqrt(jnp.sum(value * value))
    matrix = value / scale
    row = lax.broadcasted_iota(jnp.int32, value.shape, 0)
    column = lax.broadcasted_iota(jnp.int32, value.shape, 1)
    ident = jnp.where(row == column, 1.0, 0.0).astype(jnp.float32)
    current = 1.5 * ident - 0.5 * matrix
    matrix = product3(matrix, current)
    for number in range(1, NS_STEPS):
        middle = 1.5 * ident - 0.5 * product3(current, matrix)
        if number < NS_STEPS - 1:
            matrix = product3(matrix, middle)
            current = product3(middle, current)
        else:
            factor[...] = product3(middle, current[:, :size]) / jnp.sqrt(scale)

    half = near.shape[0]
    chunk = 512
    own_high, own_low = halves(factor[:size, :])
    cross_high, cross_low = halves(factor[size:, :])

    def dot(a, b):
        return jnp.dot(a, b, preferred_element_type=jnp.float32)

    def copy(index):
        rows = pl.ds(pl.multiple_of(index * chunk, chunk), chunk)
        return pltpu.make_async_copy(work.at[rows], rotated.at[rows], sems.at[index])

    per = half // chunk
    for part, other in ((me, near), (1 - me, far)):
        for turn in range(per):
            index = part * per + turn
            rows = pl.ds(pl.multiple_of(index * chunk, chunk), chunk)
            high, low = halves(exact[rows, :])
            across = other[turn * chunk:(turn + 1) * chunk, :]
            work[rows, :] = (dot(high, own_high) + dot(across, cross_high)) + (
                dot(high, own_low) + dot(low, own_high) + dot(across, cross_low)
            )
            copy(index).start()
    for index in range(2 * per):
        copy(index).wait()


def call(kernel, out, specs, scratch=(), mib=8, out_specs=None, cost=None, **more):
    return pl.pallas_call(
        kernel,
        out_shape=out,
        in_specs=specs,
        out_specs=out_specs if out_specs is not None else jax.tree.map(lambda _: VMEM, out),
        scratch_shapes=scratch,
        compiler_params=limit(mib),
        cost_estimate=cost,
        **more,
    )


def shape(rows, columns, dtype=jnp.float32):
    return jax.ShapeDtypeStruct((rows, columns), dtype)


def passed_along(value, axis, steps):
    count = lax.axis_size(axis)
    pairs = [(source, (source + steps) % count) for source in range(count)]
    return lax.ppermute(value, axis, pairs)


def sent_faces(values):
    values = values.reshape(4, -1, LANES)
    return (
        passed_along(values[0], "dx", 1),
        passed_along(values[1], "dx", -1),
        passed_along(values[2], "dy", 1),
        passed_along(values[3], "dy", -1),
    )


def sent_ghosts(values):
    values = values.reshape(4, -1, LANES)
    return (
        passed_along(values[0], "dx", -1),
        passed_along(values[1], "dx", 1),
        passed_along(values[2], "dy", -1),
        passed_along(values[3], "dy", 1),
    )


def local(orbitals, hamiltonians, connectivity, face_maps):
    field = orbitals[0, 0]
    hamiltonian = hamiltonians[0, 0]
    connection = connectivity[0, 0].reshape(-1)
    faces = 2 * face_maps[0, 0].reshape(-1)
    nodes, columns = field.shape
    wide = columns // LANES
    slots = connection.shape[0]
    face_rows = faces.shape[0]
    rows = nodes + face_rows
    cells, points, _ = hamiltonian.shape

    current, face_vals = call(
        start_kernel,
        [shape(wide * nodes, LANES), shape(wide * face_rows, LANES, jnp.bfloat16)],
        [SMEM, VMEM],
        [pltpu.VMEM((wide * face_rows, LANES), jnp.float32)],
    )(faces, field)
    received = sent_faces(face_vals)

    table = jax.ShapeDtypeStruct((rows // LANES, LANES), jnp.int32)
    one, two, extra = call(
        table_kernel,
        [table, table, jax.ShapeDtypeStruct((1,), jnp.int32)],
        [VMEM],
        out_specs=[VMEM, VMEM, SMEM],
        cost=pl.CostEstimate(flops=10**9, bytes_accessed=10**6, transcendentals=0),
    )(connection.reshape(1, -1))
    tables = (2 * connection, one.reshape(-1), two.reshape(-1), extra)

    previous = current
    for number in range(4):
        scales = (0.5, 0.25, 0.0) if number == 0 else (1.0, 0.5, 1.0)

        def cells_part(*refs, scales=scales):
            cells_kernel(scales[0], *refs)

        def owned_part(*refs, scales=scales):
            owned_kernel(scales, *refs)

        products, ghosts = call(
            cells_part,
            [shape(wide * slots + 8, LANES), shape(wide * face_rows, LANES)],
            [SMEM] * 4 + [VMEM] * 6,
            [
                pltpu.VMEM((wide * rows, LANES), jnp.float32),
                pltpu.VMEM((wide * points, LANES), jnp.float32),
            ],
            mib=12,
            cost=pl.CostEstimate(flops=2 * 10**9, bytes_accessed=10**7, transcendentals=0),
        )(*tables, current, *received, hamiltonian)
        partial = call(
            owned_part,
            shape(wide * nodes, LANES),
            [SMEM] * 4 + [VMEM] * 3,
            mib=4,
            cost=pl.CostEstimate(flops=10**9, bytes_accessed=10**7, transcendentals=0),
        )(*tables, products, current, previous)
        back = sent_ghosts(ghosts)
        if number < 3:
            previous = current
            current, face_vals = call(
                faces_kernel,
                [shape(wide * nodes, LANES), shape(wide * face_rows, LANES, jnp.bfloat16)],
                [SMEM] + [VMEM] * 5,
                [pltpu.VMEM((wide * face_rows, LANES), jnp.float32)],
                input_output_aliases={1: 0},
            )(faces, partial, *back)
            received = sent_faces(face_vals)
        else:
            band = lax.axis_index("band").astype(jnp.int32).reshape(1)
            half = shape(nodes // 2, columns, jnp.bfloat16)
            exact, mine, theirs, _ = call(
                last_kernel,
                [shape(nodes, columns), half, half, shape(wide * nodes, LANES)],
                [SMEM] * 2 + [VMEM] * 5,
                input_output_aliases={2: 3},
            )(band, faces, partial, *back)
    return finish(band, exact, mine, theirs)[None, None]


def dot_nodes(left, right):
    return lax.dot_general(left, right, (((0,), (0,)), ((), ())), preferred_element_type=jnp.float32)


def finish(band, exact, mine, theirs):
    nodes, columns = exact.shape
    domains = lax.axis_size(("dx", "dy"))
    near = passed_along(theirs, "band", 1)
    whole = dot_nodes(mine, mine) + dot_nodes(theirs, theirs)
    cross = dot_nodes(mine, near)
    far = passed_along(mine, "band", 1)
    pieces = jnp.concatenate(
        [whole[:, :LANES], whole[:, LANES:], cross[:, :LANES], cross[:, LANES:]], axis=0
    ).astype(jnp.bfloat16)
    pieces = pieces.reshape(domains, -1, LANES)
    pieces = lax.all_to_all(pieces, ("dx", "dy"), 0, 0, tiled=True)
    scale = 1.0 / (nodes * domains)

    def kernel(*refs):
        sum_kernel(scale, *refs)

    devices = lax.axis_size(("band", "dx", "dy"))
    sums = call(kernel, jax.ShapeDtypeStruct((devices, *pieces.shape[1:]), jnp.bfloat16), [VMEM], mib=4)(pieces)
    sums = lax.all_to_all(sums, ("band", "dx", "dy"), 0, 0, tiled=True)
    blocks = sums.reshape(2, -1, LANES)
    return call(
        rotate_kernel,
        shape(nodes, columns),
        [SMEM] + [VMEM] * 4,
        [
            pltpu.VMEM((2 * columns, columns), jnp.float32),
            pltpu.VMEM((nodes, columns), jnp.float32),
            pltpu.SemaphoreType.DMA((nodes // 512,)),
        ],
        mib=24,
        out_specs=pl.BlockSpec(memory_space=pl.ANY),
    )(band, blocks, exact, near, far)


def solution(mesh):
    in_specs = (
        P("dx", "dy", None, "band"),
        P("dx", "dy", None, None, None),
        P("dx", "dy", None, None),
        P("dx", "dy", None, None),
    )
    out_specs = P("dx", "dy", None, "band")
    return jax.shard_map(local, mesh=mesh, in_specs=in_specs, out_specs=out_specs, check_vma=False)
```

time: 330 us -> 247 us (0.75); the launches traced: 330 us -> 242 us
  waiting for transfers between devices: 70.1 us -> 35.6 us
  local copies, waits for them, and re-layouts: 32 us -> 13.3 us
  other arithmetic: 13.5 us -> 1.47 us
  Pallas kernels: 121 us -> 111 us
  matrix products: 11.1 us -> 4.14 us
    ppermute x34, waiting for transfers between devices: 44.9 us -> 25.2 us  [passed_along(): return lax.ppermute(value, axis, pairs)]
    all_to_all x1, waiting for transfers between devices: 25.3 us -> 10.4 us  [finish(): sums = lax.all_to_all(sums, ('band', 'dx', 'dy'), 0, 0, tiled=True)]
    unnamed x37 -> x21, local copies, waits for them, and re-layouts: 22.5 us -> 11.9 us
    pallas_call x7 -> x12, Pallas kernels: 107 us -> 98.2 us  [the longest x4 50.7 us: local(): call(cells_part, [shape(wide * slots + 8, LANES), shape(wide * face_rows,...]
    dot_general x2 -> x0, matrix products: 6.82 us -> none  [the longest x1 4.37 us: finish(): jnp.dot(exact, own, precision=lax.Precision.HIGHEST)]
    convert_element_type x1 -> x0, other arithmetic: 4.61 us -> none  [summed(): pieces = value.astype(jnp.bfloat16).reshape(count, -1)]
    div x1 -> x0, other arithmetic: 4.32 us -> none  [finish(): block = summed(block, ('dx', 'dy', 'band')) / total]
    ppermute x34, starting transfers between devices: 48.8 us -> 44.9 us  [passed_along(): return lax.ppermute(value, axis, pairs)]
  transfers between devices with their start and end apart: 35 -> 35, of which waited for: 18 -> 9; matrix products, arithmetic and copies ran while one was open for 4% -> 2% of each run, Pallas kernels for 8% -> 13%
where the time goes in v2:
time: 247 us; the launch traced here: 242 us
  Pallas kernels  111 us (45%)
  starting transfers between devices  55.2 us (22%)
  waiting for transfers between devices  35.6 us (14%)
  blocking collectives  20.6 us (8%)
  local copies, waits for them, and re-layouts  13.3 us (5%)
  matrix products  4.14 us (2%)
    pallas_call x4, Pallas kernels, local(): call(cells_part, [shape(wide * slots + 8, LANES), shape(wide * face_rows,...  50.7 us
    ppermute x34, starting transfers between devices, passed_along(): return lax.ppermute(value, axis, pairs)  44.9 us
    pallas_call x4, Pallas kernels, local(): call(owned_part, shape(wide * nodes, LANES), [SMEM] * 4 + [VMEM] * 3, mib...  27.6 us
    ppermute x34, waiting for transfers between devices, passed_along(): return lax.ppermute(value, axis, pairs)  25.2 us
    all_to_all x1, blocking collectives, finish(): pieces = lax.all_to_all(pieces, ('dx', 'dy'), 0, 0, tiled=True)  20.6 us
    unnamed x21, local copies, waits for them, and re-layouts  11.9 us
    pallas_call x3, Pallas kernels, local(): call(faces_kernel, [shape(wide * nodes, LANES), shape(wide * face_rows, L...  11.5 us
    pallas_call x1, Pallas kernels, finish(): call(rotate_kernel, shape(nodes, columns), [SMEM] + [VMEM] * 4, [pltpu.VM...  11.1 us
  transfers between devices with their start and end apart: 35, of which 9 were waited for; matrix products, arithmetic and copies ran while one was open for 2% of the time, Pallas kernels for 13%

profile of v2, /device:TPU:19, one launch (start us, length us, event | category | flops | bytes accessed | tf_op | source)
XLA Modules:
  0.0 242.4 jit_solution(17621074779659599264)
XLA Ops:
  0.0 0.7 multiply_bitcast_fusion
  0.7 1.9 copy-done.5
  2.6 1.8 shard_map.47
  4.4 1.3 collective-permute-start
  5.7 0.3 collective-permute-start.1
  6.0 2.8 %collective-permute-start.2 = (bf16[512,128]{1,0:T(8,128)(2,1)S(1)}, bf16[512,128]{1,0:T(8,128)(2,1)S(1)}, u32[]{:S(2)}, u32[]{:S(2)}) collective-permute-start(bf16[512,128]{1,0:T(8,128)(2,1)S(1)} %get-tuple-element.78), channel_id=1, source_target_pairs={{0,2},{2,4},{4,6},{6,8},{8,10},{10,12},{12,14},{14,0},{1,3},{3,5},... | collective-permute-start | bytes 393224 | tf_op jit(solution)/shard_map/ppermute | solution.py:325
  8.7 0.8 broadcast_multiply_fusion
  9.5 0.7 copy-done.9
  10.2 4.1 %shard_map.46 = (s32[32,128]{1,0:T(8,128)S(1)}, s32[32,128]{1,0:T(8,128)S(1)}, s32[1]{0:T(128)}) custom-call(s32[1,6144]{1,0:T(1,128)S(1)} %bitcast.53), custom_call_target="tpu_custom_call" | custom-call | flops 1000000000 | bytes 1000000 | tf_op jit(solution)/shard_map/pallas_call | solution.py:369
  14.4 12.7 %shard_map.48 = (f32[12296,128]{1,0:T(8,128)S(1)}, f32[2048,128]{1,0:T(8,128)S(1)}) custom-call(s32[6144]{0:T(1024)S(1)} %bitcast.24, s32[4096]{0:T(1024)S(1)} %bitcast.32, s32[4096]{0:T(1024)S(1)} %bitcast.40, s32[1]{0:T(128)} %get-tuple-element.29.refs_3_, f32[6144,128]{1,0:T(8,128)S(1)} %get-tuple-element.30.refs_4_.refs_5_.refs_6_, ...), custom_call_target="tpu_custom_call" | custom-call | flops 2000000000 | bytes 10000000 | tf_op jit(solution)/shard_map/pallas_call | solution.py:388
  27.2 2.4 %collective-permute-start.4 = (f32[512,128]{1,0:T(8,128)S(1)}, f32[512,128]{1,0:T(8,128)S(1)}, u32[]{:S(2)}, u32[]{:S(2)}) collective-permute-start(f32[512,128]{1,0:T(8,128)S(1)} %get-tuple-element.64), channel_id=1, source_target_pairs={{0,112},{16,0},{32,16},{48,32},{64,48},{80,64},{96,80},{112,96},{1... | collective-permute-start | bytes 786440 | tf_op jit(solution)/shard_map/ppermute | solution.py:325
  29.7 1.7 collective-permute-start.6
  31.4 0.3 collective-permute-start.7
  31.7 6.7 %shard_map.49.partial = f32[6144,128]{1,0:T(8,128)S(1)} custom-call(s32[6144]{0:T(1024)S(1)} %bitcast.25, s32[4096]{0:T(1024)S(1)} %bitcast.33, s32[4096]{0:T(1024)S(1)} %bitcast.41, s32[1]{0:T(128)} %get-tuple-element.29.refs_3_, f32[12296,128]{1,0:T(8,128)S(1)} %get-tuple-element.32.refs_4_, f32[6144,128]{1,0:T(8,128)S(1)} %get-tuple-element.30.refs_4_.refs_5_.refs_6_, ...), custom_call_target="tpu_custom_call" | custom-call | flops 1000000000 | bytes 10000000 | tf_op jit(solution)/shard_map/pallas_call | solution.py:399
  38.4 3.8 %shard_map.50 = (f32[6144,128]{1,0:T(8,128)S(1)}, bf16[2048,128]{1,0:T(8,128)(2,1)S(1)}) custom-call(s32[1024]{0:T(1024)S(1)} %bitcast.49, f32[6144,128]{1,0:T(8,128)S(1)} %shard_map.49.partial, f32[512,128]{1,0:T(8,128)S(1)} %collective-permute-done.4.west, f32[512,128]{1,0:T(8,128)S(1)} %collective-permute-done.5.east, ...), custom_call_target="tpu_custom_call", output_to_operand_aliasing={{0}: (1, {})} | custom-call | tf_op jit(solution)/shard_map/pallas_call | solution.py:409
  42.3 1.5 collective-permute-start.10
  43.8 3.2 %collective-permute-start.9 = (bf16[512,128]{1,0:T(8,128)(2,1)S(1)}, bf16[512,128]{1,0:T(8,128)(2,1)S(1)}, u32[]{:S(2)}, u32[]{:S(2)}) collective-permute-start(bf16[512,128]{1,0:T(8,128)(2,1)S(1)} %get-tuple-element.75), channel_id=1, source_target_pairs={{0,112},{16,0},{32,16},{48,32},{64,48},{80,64},{96,80},{112,96},{1... | collective-permute-start | bytes 393224 | tf_op jit(solution)/shard_map/ppermute | solution.py:325
  47.0 1.4 collective-permute-done.11.refs_8_
  48.4 1.0 collective-permute-done.8.refs_5_
  49.3 12.7 %shard_map.51 = (f32[12296,128]{1,0:T(8,128)S(1)}, f32[2048,128]{1,0:T(8,128)S(1)}) custom-call(s32[6144]{0:T(1024)S(1)} %bitcast.26, s32[4096]{0:T(1024)S(1)} %bitcast.34, s32[4096]{0:T(1024)S(1)} %bitcast.42, s32[1]{0:T(128)} %get-tuple-element.29.refs_3_, f32[6144,128]{1,0:T(8,128)S(1)} %get-tuple-element.34.refs_4_.refs_5_.refs_6_, ...), custom_call_target="tpu_custom_call" | custom-call | flops 2000000000 | bytes 10000000 | tf_op jit(solution)/shard_map/pallas_call | solution.py:388
  62.1 3.6 %collective-permute-start.12 = (f32[512,128]{1,0:T(8,128)S(1)}, f32[512,128]{1,0:T(8,128)S(1)}, u32[]{:S(2)}, u32[]{:S(2)}) collective-permute-start(f32[512,128]{1,0:T(8,128)S(1)} %get-tuple-element.60), channel_id=1, source_target_pairs={{0,112},{16,0},{32,16},{48,32},{64,48},{80,64},{96,80},{112,96},{1... | collective-permute-start | bytes 786440 | tf_op jit(solution)/shard_map/ppermute | solution.py:325
  65.7 2.9 %collective-permute-start.14 = (f32[512,128]{1,0:T(8,128)S(1)}, f32[512,128]{1,0:T(8,128)S(1)}, u32[]{:S(2)}, u32[]{:S(2)}) collective-permute-start(f32[512,128]{1,0:T(8,128)S(1)} %get-tuple-element.58), channel_id=1, source_target_pairs={{0,14},{2,0},{4,2},{6,4},{8,6},{10,8},{12,10},{14,12},{1,15},{3,1}... | collective-permute-start | bytes 786440 | tf_op jit(solution)/shard_map/ppermute | solution.py:325
  68.6 0.7 collective-permute-start.15
  69.3 6.8 %shard_map.52.partial = f32[6144,128]{1,0:T(8,128)S(1)} custom-call(s32[6144]{0:T(1024)S(1)} %bitcast.27, s32[4096]{0:T(1024)S(1)} %bitcast.35, s32[4096]{0:T(1024)S(1)} %bitcast.43, s32[1]{0:T(128)} %get-tuple-element.29.refs_3_, f32[12296,128]{1,0:T(8,128)S(1)} %get-tuple-element.36.refs_4_, f32[6144,128]{1,0:T(8,128)S(1)} %get-tuple-element.34.refs_4_.refs_5_.refs_6_, ...), custom_call_target="tpu_custom_call" | custom-call | flops 1000000000 | bytes 10000000 | tf_op jit(solution)/shard_map/pallas_call | solution.py:399
  76.2 3.8 %shard_map.53 = (f32[6144,128]{1,0:T(8,128)S(1)}, bf16[2048,128]{1,0:T(8,128)(2,1)S(1)}) custom-call(s32[1024]{0:T(1024)S(1)} %bitcast.50, f32[6144,128]{1,0:T(8,128)S(1)} %shard_map.52.partial, f32[512,128]{1,0:T(8,128)S(1)} %collective-permute-done.12.west, f32[512,128]{1,0:T(8,128)S(1)} %collective-permute-done.13.east, ...), custom_call_target="tpu_custom_call", output_to_operand_aliasing={{0}: (1, {})} | custom-call | tf_op jit(solution)/shard_map/pallas_call | solution.py:409
  80.1 2.4 collective-permute-start.16
  82.5 1.3 collective-permute-start.17
  83.8 2.3 collective-permute-start.18
  86.1 0.3 collective-permute-done.16.refs_5_
  86.4 3.4 %collective-permute-done.17.refs_6_ = bf16[512,128]{1,0:T(8,128)(2,1)S(1)} collective-permute-done((bf16[512,128]{1,0:T(8,128)(2,1)S(1)}, bf16[512,128]{1,0:T(8,128)(2,1)S(1)}, u32[]{:S(2)}, u32[]{:S(2)}) %collective-permute-start.17) | collective-permute-done | bytes 131104 | tf_op jit(solution)/shard_map/ppermute | solution.py:325
  89.8 0.7 collective-permute-done.19.refs_8_
  90.5 12.7 %shard_map.54 = (f32[12296,128]{1,0:T(8,128)S(1)}, f32[2048,128]{1,0:T(8,128)S(1)}) custom-call(s32[6144]{0:T(1024)S(1)} %bitcast.28, s32[4096]{0:T(1024)S(1)} %bitcast.36, s32[4096]{0:T(1024)S(1)} %bitcast.44, s32[1]{0:T(128)} %get-tuple-element.29.refs_3_, f32[6144,128]{1,0:T(8,128)S(1)} %get-tuple-element.38.refs_4_.refs_5_.refs_6_, ...), custom_call_target="tpu_custom_call" | custom-call | flops 2000000000 | bytes 10000000 | tf_op jit(solution)/shard_map/pallas_call | solution.py:388
  103.3 3.8 %collective-permute-start.20 = (f32[512,128]{1,0:T(8,128)S(1)}, f32[512,128]{1,0:T(8,128)S(1)}, u32[]{:S(2)}, u32[]{:S(2)}) collective-permute-start(f32[512,128]{1,0:T(8,128)S(1)} %get-tuple-element.56), channel_id=1, source_target_pairs={{0,112},{16,0},{32,16},{48,32},{64,48},{80,64},{96,80},{112,96},{1... | collective-permute-start | bytes 786440 | tf_op jit(solution)/shard_map/ppermute | solution.py:325
  107.1 0.6 collective-permute-start.22
  107.7 1.1 collective-permute-start.23
  108.9 6.8 %shard_map.55.partial = f32[6144,128]{1,0:T(8,128)S(1)} custom-call(s32[6144]{0:T(1024)S(1)} %bitcast.29, s32[4096]{0:T(1024)S(1)} %bitcast.37, s32[4096]{0:T(1024)S(1)} %bitcast.45, s32[1]{0:T(128)} %get-tuple-element.29.refs_3_, f32[12296,128]{1,0:T(8,128)S(1)} %get-tuple-element.40.refs_4_, f32[6144,128]{1,0:T(8,128)S(1)} %get-tuple-element.38.refs_4_.refs_5_.refs_6_, ...), custom_call_target="tpu_custom_call" | custom-call | flops 1000000000 | bytes 10000000 | tf_op jit(solution)/shard_map/pallas_call | solution.py:399
  115.7 3.8 %shard_map.56 = (f32[6144,128]{1,0:T(8,128)S(1)}, bf16[2048,128]{1,0:T(8,128)(2,1)S(1)}) custom-call(s32[1024]{0:T(1024)S(1)} %bitcast.51, f32[6144,128]{1,0:T(8,128)S(1)} %shard_map.55.partial, f32[512,128]{1,0:T(8,128)S(1)} %collective-permute-done.20.west, f32[512,128]{1,0:T(8,128)S(1)} %collective-permute-done.21.east, ...), custom_call_target="tpu_custom_call", output_to_operand_aliasing={{0}: (1, {})} | custom-call | tf_op jit(solution)/shard_map/pallas_call | solution.py:409
  119.7 1.5 collective-permute-start.25
  121.2 2.6 %collective-permute-start.26 = (bf16[512,128]{1,0:T(8,128)(2,1)S(1)}, bf16[512,128]{1,0:T(8,128)(2,1)S(1)}, u32[]{:S(2)}, u32[]{:S(2)}) collective-permute-start(bf16[512,128]{1,0:T(8,128)(2,1)S(1)} %get-tuple-element.66), channel_id=1, source_target_pairs={{0,2},{2,4},{4,6},{6,8},{8,10},{10,12},{12,14},{14,0},{1,3},{3,5},... | collective-permute-start | bytes 393224 | tf_op jit(solution)/shard_map/ppermute | solution.py:325
  123.8 2.0 collective-permute-done.25.refs_6_
  125.9 2.7 %collective-permute-done.27.refs_8_ = bf16[512,128]{1,0:T(8,128)(2,1)S(1)} collective-permute-done((bf16[512,128]{1,0:T(8,128)(2,1)S(1)}, bf16[512,128]{1,0:T(8,128)(2,1)S(1)}, u32[]{:S(2)}, u32[]{:S(2)}) %collective-permute-start.27) | collective-permute-done | bytes 131104 | tf_op jit(solution)/shard_map/ppermute | solution.py:325
  128.5 12.7 %shard_map.57 = (f32[12296,128]{1,0:T(8,128)S(1)}, f32[2048,128]{1,0:T(8,128)S(1)}) custom-call(s32[6144]{0:T(1024)S(1)} %bitcast.30, s32[4096]{0:T(1024)S(1)} %bitcast.38, s32[4096]{0:T(1024)S(1)} %bitcast.46, s32[1]{0:T(128)} %get-tuple-element.29.refs_3_, f32[6144,128]{1,0:T(8,128)S(1)} %get-tuple-element.42.refs_4_.refs_5_, ...), custom_call_target="tpu_custom_call" | custom-call | flops 2000000000 | bytes 10000000 | tf_op jit(solution)/shard_map/pallas_call | solution.py:388
  141.2 2.6 %copy-done.3 = f32[12296,128]{1,0:T(8,128)} copy-done((f32[12296,128]{1,0:T(8,128)}, f32[12296,128]{1,0:T(8,128)S(1)}, u32[]{:S(2)}) %copy-start.3) | copy-done | bytes 6295576
  143.9 1.0 fusion.1
  144.9 3.6 %collective-permute-start.28 = (f32[512,128]{1,0:T(8,128)}, f32[512,128]{1,0:T(8,128)S(1)}, u32[]{:S(2)}, u32[]{:S(2)}) collective-permute-start(f32[512,128]{1,0:T(8,128)} %get-tuple-element.52), channel_id=1, source_target_pairs={{0,112},{16,0},{32,16},{48,32},{64,48},{80,64},{96,80},{112,96},{1... | collective-permute-start | bytes 786440 | tf_op jit(solution)/shard_map/ppermute | solution.py:325
  148.5 0.7 collective-permute-start.30
  149.2 1.1 collective-permute-start.31
  150.3 1.9 copy-done.2
  152.1 2.8 %copy-done.4 = f32[12296,128]{1,0:T(8,128)S(1)} copy-done((f32[12296,128]{1,0:T(8,128)S(1)}, f32[12296,128]{1,0:T(8,128)}, u32[]{:S(2)}) %copy-start.4) | copy-done | bytes 6295576
  154.9 7.3 %shard_map.58.partial = f32[6144,128]{1,0:T(8,128)S(1)} custom-call(s32[6144]{0:T(1024)S(1)} %bitcast.31, s32[4096]{0:T(1024)S(1)} %bitcast.39, s32[4096]{0:T(1024)S(1)} %bitcast.47, s32[1]{0:T(128)} %get-tuple-element.29.refs_3_, f32[12296,128]{1,0:T(8,128)S(1)} %copy-done.4, f32[6144,128]{1,0:T(8,128)S(1)} %copy-done.2, ...), custom_call_target="tpu_custom_call" | custom-call | flops 1000000000 | bytes 10000000 | tf_op jit(solution)/shard_map/pallas_call | solution.py:399
  162.2 4.6 %shard_map.59 = (f32[3072,256]{1,0:T(8,128)S(1)}, bf16[1536,256]{1,0:T(8,128)(2,1)}, bf16[1536,256]{1,0:T(8,128)(2,1)S(1)}, f32[6144,128]{1,0:T(8,128)S(1)}) custom-call(s32[1]{0:T(128)} %bitcast.band, s32[1024]{0:T(1024)S(1)} %bitcast.52, f32[6144,128]{1,0:T(8,128)S(1)} %shard_map.58.partial, ...), custom_call_target="tpu_custom_call", output_to_operand_aliasing={{3}: (2, {})} | custom-call | tf_op jit(solution)/shard_map/pallas_call | solution.py:420
  166.9 0.3 collective-permute-start.32
  167.2 2.6 %collective-permute-start.33 = (bf16[1536,256]{1,0:T(8,128)(2,1)}, bf16[1536,256]{1,0:T(8,128)(2,1)}, u32[]{:S(2)}, u32[]{:S(2)}) collective-permute-start(bf16[1536,256]{1,0:T(8,128)(2,1)} %get-tuple-element.46), channel_id=1, source_target_pairs={{0,1},{1,0},{2,3},{3,2},{4,5},{5,4},{6,7},{7,6},{8,9},{9,8},{10,11... | collective-permute-start | bytes 2359304 | tf_op jit(solution)/shard_map/ppermute | solution.py:325
  169.9 0.4 fusion.11
  170.3 1.9 fusion
  172.2 13.7 %collective-permute-done.32.near = bf16[1536,256]{1,0:T(8,128)(2,1)S(1)} collective-permute-done((bf16[1536,256]{1,0:T(8,128)(2,1)S(1)}, bf16[1536,256]{1,0:T(8,128)(2,1)S(1)}, u32[]{:S(2)}, u32[]{:S(2)}) %collective-permute-start.32) | collective-permute-done | bytes 786464 | tf_op jit(solution)/shard_map/ppermute | solution.py:325
  185.9 1.8 convolution_convert_fusion
  187.8 20.6 %all_to_all.10.refs_0_ = bf16[64,16,128]{2,1,0:T(8,128)(2,1)S(1)} all-to-all(bf16[64,16,128]{2,1,0:T(8,128)(2,1)S(1)} %bitcast.54), channel_id=1, replica_groups=mesh['dx'=8,'dy'=8,'band'=2] {'dx','dy'}, dimensions={0} | all-to-all | bytes 524288 | tf_op jit(solution)/shard_map/all_to_all | solution.py:444
  208.4 0.1 shard_map.60
  208.5 0.8 copy-done.6
  209.3 10.3 %all-to-all-start.1 = ((bf16[128,16,128]{2,1,0:T(8,128)(2,1)}), bf16[128,16,128]{2,1,0:T(8,128)(2,1)}, u32[]{:S(2)}, u32[]{:S(2)}) async-start(bf16[128,16,128]{2,1,0:T(8,128)(2,1)} %copy-done.6), calls=%async_computation.1 | async-start | bytes 1048576 | tf_op jit(solution)/shard_map/all_to_all | solution.py:452
  219.6 10.4 %all-to-all-done.1 = bf16[128,16,128]{2,1,0:T(8,128)(2,1)} async-done(((bf16[128,16,128]{2,1,0:T(8,128)(2,1)}), bf16[128,16,128]{2,1,0:T(8,128)(2,1)}, u32[]{:S(2)}, u32[]{:S(2)}) %all-to-all-start.1) | async-done | bytes 524320 | tf_op jit(solution)/shard_map/all_to_all | solution.py:452
  230.0 1.1 copy-done.8
  231.2 11.1 %shard_map.61 = f32[3072,256]{1,0:T(8,128)} custom-call(s32[1]{0:T(128)} %bitcast.band, bf16[2,1024,128]{2,1,0:T(8,128)(2,1)} %bitcast.8.blocks, f32[3072,256]{1,0:T(8,128)S(1)} %get-tuple-element.48.exact, bf16[1536,256]{1,0:T(8,128)(2,1)S(1)} %copy-done.8, bf16[1536,256]{1,0:T(8,128)(2,1)} %collective-permute-done.33.far), custom_call_target="tpu_custom_call" | custom-call | tf_op jit(solution)/shard_map/pallas_call | solution.py:454
  (60 shorter events, 0.6 us)
Async XLA Ops:
  0.7 1.9 copy-start.5
  2.6 11.8 %copy-start = (bf16[1,1,12,512,512]{4,3,2,1,0:T(8,128)(2,1)S(1)}, bf16[1,1,12,512,512]{4,3,2,1,0:T(8,128)(2,1)}, u32[]{:S(2)}) copy-start(bf16[1,1,12,512,512]{4,3,2,1,0:T(8,128)(2,1)} %param.5) | copy-start | bytes 18874372
  4.4 9.9 %collective-permute-start = (bf16[512,128]{1,0:T(8,128)(2,1)S(1)}, bf16[512,128]{1,0:T(8,128)(2,1)S(1)}, u32[]{:S(2)}, u32[]{:S(2)}) collective-permute-start(bf16[512,128]{1,0:T(8,128)(2,1)S(1)} %get-tuple-element.80), channel_id=1, source_target_pairs={{0,16},{16,32},{32,48},{48,64},{64,80},{80,96},{96,112},{112,0},{1... | collective-permute-start | bytes 393224 | tf_op jit(solution)/shard_map/ppermute | solution.py:325
  5.7 8.6 %collective-permute-start.1 = (bf16[512,128]{1,0:T(8,128)(2,1)S(1)}, bf16[512,128]{1,0:T(8,128)(2,1)S(1)}, u32[]{:S(2)}, u32[]{:S(2)}) collective-permute-start(bf16[512,128]{1,0:T(8,128)(2,1)S(1)} %get-tuple-element.79), channel_id=1, source_target_pairs={{0,112},{16,0},{32,16},{48,32},{64,48},{80,64},{96,80},{112,96},{1... | collective-permute-start | bytes 393224 | tf_op jit(solution)/shard_map/ppermute | solution.py:325
  6.0 8.4 %collective-permute-start.2 = (bf16[512,128]{1,0:T(8,128)(2,1)S(1)}, bf16[512,128]{1,0:T(8,128)(2,1)S(1)}, u32[]{:S(2)}, u32[]{:S(2)}) collective-permute-start(bf16[512,128]{1,0:T(8,128)(2,1)S(1)} %get-tuple-element.78), channel_id=1, source_target_pairs={{0,2},{2,4},{4,6},{6,8},{8,10},{10,12},{12,14},{14,0},{1,3},{3,5},... | collective-permute-start | bytes 393224 | tf_op jit(solution)/shard_map/ppermute | solution.py:325
  8.7 5.7 %collective-permute-start.3 = (bf16[512,128]{1,0:T(8,128)(2,1)S(1)}, bf16[512,128]{1,0:T(8,128)(2,1)S(1)}, u32[]{:S(2)}, u32[]{:S(2)}) collective-permute-start(bf16[512,128]{1,0:T(8,128)(2,1)S(1)} %get-tuple-element.77), channel_id=1, source_target_pairs={{0,14},{2,0},{4,2},{6,4},{8,6},{10,8},{12,10},{14,12},{1,15},{3,1}... | collective-permute-start | bytes 393224 | tf_op jit(solution)/shard_map/ppermute | solution.py:325
  9.5 0.7 copy-start.9
  27.2 11.2 %collective-permute-start.4 = (f32[512,128]{1,0:T(8,128)S(1)}, f32[512,128]{1,0:T(8,128)S(1)}, u32[]{:S(2)}, u32[]{:S(2)}) collective-permute-start(f32[512,128]{1,0:T(8,128)S(1)} %get-tuple-element.64), channel_id=1, source_target_pairs={{0,112},{16,0},{32,16},{48,32},{64,48},{80,64},{96,80},{112,96},{1... | collective-permute-start | bytes 786440 | tf_op jit(solution)/shard_map/ppermute | solution.py:325
  29.7 8.7 %collective-permute-start.5 = (f32[512,128]{1,0:T(8,128)S(1)}, f32[512,128]{1,0:T(8,128)S(1)}, u32[]{:S(2)}, u32[]{:S(2)}) collective-permute-start(f32[512,128]{1,0:T(8,128)S(1)} %get-tuple-element.63), channel_id=1, source_target_pairs={{0,16},{16,32},{32,48},{48,64},{64,80},{80,96},{96,112},{112,0},{1... | collective-permute-start | bytes 786440 | tf_op jit(solution)/shard_map/ppermute | solution.py:325
  29.7 8.8 %collective-permute-start.6 = (f32[512,128]{1,0:T(8,128)S(1)}, f32[512,128]{1,0:T(8,128)S(1)}, u32[]{:S(2)}, u32[]{:S(2)}) collective-permute-start(f32[512,128]{1,0:T(8,128)S(1)} %get-tuple-element.62), channel_id=1, source_target_pairs={{0,14},{2,0},{4,2},{6,4},{8,6},{10,8},{12,10},{14,12},{1,15},{3,1}... | collective-permute-start | bytes 786440 | tf_op jit(solution)/shard_map/ppermute | solution.py:325
  31.4 7.0 %collective-permute-start.7 = (f32[512,128]{1,0:T(8,128)S(1)}, f32[512,128]{1,0:T(8,128)S(1)}, u32[]{:S(2)}, u32[]{:S(2)}) collective-permute-start(f32[512,128]{1,0:T(8,128)S(1)} %get-tuple-element.61), channel_id=1, source_target_pairs={{0,2},{2,4},{4,6},{6,8},{8,10},{10,12},{12,14},{14,0},{1,3},{3,5},... | collective-permute-start | bytes 786440 | tf_op jit(solution)/shard_map/ppermute | solution.py:325
  42.3 4.7 %collective-permute-start.10 = (bf16[512,128]{1,0:T(8,128)(2,1)S(1)}, bf16[512,128]{1,0:T(8,128)(2,1)S(1)}, u32[]{:S(2)}, u32[]{:S(2)}) collective-permute-start(bf16[512,128]{1,0:T(8,128)(2,1)S(1)} %get-tuple-element.74), channel_id=1, source_target_pairs={{0,2},{2,4},{4,6},{6,8},{8,10},{10,12},{12,14},{14,0},{1,3},{3,5},... | collective-permute-start | bytes 393224 | tf_op jit(solution)/shard_map/ppermute | solution.py:325
  43.8 4.6 %collective-permute-start.11 = (bf16[512,128]{1,0:T(8,128)(2,1)S(1)}, bf16[512,128]{1,0:T(8,128)(2,1)S(1)}, u32[]{:S(2)}, u32[]{:S(2)}) collective-permute-start(bf16[512,128]{1,0:T(8,128)(2,1)S(1)} %get-tuple-element.73), channel_id=1, source_target_pairs={{0,14},{2,0},{4,2},{6,4},{8,6},{10,8},{12,10},{14,12},{1,15},{3,1}... | collective-permute-start | bytes 393224 | tf_op jit(solution)/shard_map/ppermute | solution.py:325
  43.8 5.5 %collective-permute-start.8 = (bf16[512,128]{1,0:T(8,128)(2,1)S(1)}, bf16[512,128]{1,0:T(8,128)(2,1)S(1)}, u32[]{:S(2)}, u32[]{:S(2)}) collective-permute-start(bf16[512,128]{1,0:T(8,128)(2,1)S(1)} %get-tuple-element.76), channel_id=1, source_target_pairs={{0,16},{16,32},{32,48},{48,64},{64,80},{80,96},{96,112},{112,0},{1... | collective-permute-start | bytes 393224 | tf_op jit(solution)/shard_map/ppermute | solution.py:325
  43.8 5.5 %collective-permute-start.9 = (bf16[512,128]{1,0:T(8,128)(2,1)S(1)}, bf16[512,128]{1,0:T(8,128)(2,1)S(1)}, u32[]{:S(2)}, u32[]{:S(2)}) collective-permute-start(bf16[512,128]{1,0:T(8,128)(2,1)S(1)} %get-tuple-element.75), channel_id=1, source_target_pairs={{0,112},{16,0},{32,16},{48,32},{64,48},{80,64},{96,80},{112,96},{1... | collective-permute-start | bytes 393224 | tf_op jit(solution)/shard_map/ppermute | solution.py:325
  62.1 14.1 %collective-permute-start.12 = (f32[512,128]{1,0:T(8,128)S(1)}, f32[512,128]{1,0:T(8,128)S(1)}, u32[]{:S(2)}, u32[]{:S(2)}) collective-permute-start(f32[512,128]{1,0:T(8,128)S(1)} %get-tuple-element.60), channel_id=1, source_target_pairs={{0,112},{16,0},{32,16},{48,32},{64,48},{80,64},{96,80},{112,96},{1... | collective-permute-start | bytes 786440 | tf_op jit(solution)/shard_map/ppermute | solution.py:325
  65.7 10.4 %collective-permute-start.13 = (f32[512,128]{1,0:T(8,128)S(1)}, f32[512,128]{1,0:T(8,128)S(1)}, u32[]{:S(2)}, u32[]{:S(2)}) collective-permute-start(f32[512,128]{1,0:T(8,128)S(1)} %get-tuple-element.59), channel_id=1, source_target_pairs={{0,16},{16,32},{32,48},{48,64},{64,80},{80,96},{96,112},{112,0},{1... | collective-permute-start | bytes 786440 | tf_op jit(solution)/shard_map/ppermute | solution.py:325
  65.7 10.4 %collective-permute-start.14 = (f32[512,128]{1,0:T(8,128)S(1)}, f32[512,128]{1,0:T(8,128)S(1)}, u32[]{:S(2)}, u32[]{:S(2)}) collective-permute-start(f32[512,128]{1,0:T(8,128)S(1)} %get-tuple-element.58), channel_id=1, source_target_pairs={{0,14},{2,0},{4,2},{6,4},{8,6},{10,8},{12,10},{14,12},{1,15},{3,1}... | collective-permute-start | bytes 786440 | tf_op jit(solution)/shard_map/ppermute | solution.py:325
  68.6 7.6 %collective-permute-start.15 = (f32[512,128]{1,0:T(8,128)S(1)}, f32[512,128]{1,0:T(8,128)S(1)}, u32[]{:S(2)}, u32[]{:S(2)}) collective-permute-start(f32[512,128]{1,0:T(8,128)S(1)} %get-tuple-element.57), channel_id=1, source_target_pairs={{0,2},{2,4},{4,6},{6,8},{8,10},{10,12},{12,14},{14,0},{1,3},{3,5},... | collective-permute-start | bytes 786440 | tf_op jit(solution)/shard_map/ppermute | solution.py:325
  80.1 6.4 %collective-permute-start.16 = (bf16[512,128]{1,0:T(8,128)(2,1)S(1)}, bf16[512,128]{1,0:T(8,128)(2,1)S(1)}, u32[]{:S(2)}, u32[]{:S(2)}) collective-permute-start(bf16[512,128]{1,0:T(8,128)(2,1)S(1)} %get-tuple-element.72), channel_id=1, source_target_pairs={{0,16},{16,32},{32,48},{48,64},{64,80},{80,96},{96,112},{112,0},{1... | collective-permute-start | bytes 393224 | tf_op jit(solution)/shard_map/ppermute | solution.py:325
  82.5 7.3 %collective-permute-start.17 = (bf16[512,128]{1,0:T(8,128)(2,1)S(1)}, bf16[512,128]{1,0:T(8,128)(2,1)S(1)}, u32[]{:S(2)}, u32[]{:S(2)}) collective-permute-start(bf16[512,128]{1,0:T(8,128)(2,1)S(1)} %get-tuple-element.71), channel_id=1, source_target_pairs={{0,112},{16,0},{32,16},{48,32},{64,48},{80,64},{96,80},{112,96},{1... | collective-permute-start | bytes 393224 | tf_op jit(solution)/shard_map/ppermute | solution.py:325
  83.8 6.0 %collective-permute-start.18 = (bf16[512,128]{1,0:T(8,128)(2,1)S(1)}, bf16[512,128]{1,0:T(8,128)(2,1)S(1)}, u32[]{:S(2)}, u32[]{:S(2)}) collective-permute-start(bf16[512,128]{1,0:T(8,128)(2,1)S(1)} %get-tuple-element.70), channel_id=1, source_target_pairs={{0,2},{2,4},{4,6},{6,8},{8,10},{10,12},{12,14},{14,0},{1,3},{3,5},... | collective-permute-start | bytes 393224 | tf_op jit(solution)/shard_map/ppermute | solution.py:325
  86.1 4.4 %collective-permute-start.19 = (bf16[512,128]{1,0:T(8,128)(2,1)S(1)}, bf16[512,128]{1,0:T(8,128)(2,1)S(1)}, u32[]{:S(2)}, u32[]{:S(2)}) collective-permute-start(bf16[512,128]{1,0:T(8,128)(2,1)S(1)} %get-tuple-element.69), channel_id=1, source_target_pairs={{0,14},{2,0},{4,2},{6,4},{8,6},{10,8},{12,10},{14,12},{1,15},{3,1}... | collective-permute-start | bytes 393224 | tf_op jit(solution)/shard_map/ppermute | solution.py:325
  103.3 12.4 %collective-permute-start.20 = (f32[512,128]{1,0:T(8,128)S(1)}, f32[512,128]{1,0:T(8,128)S(1)}, u32[]{:S(2)}, u32[]{:S(2)}) collective-permute-start(f32[512,128]{1,0:T(8,128)S(1)} %get-tuple-element.56), channel_id=1, source_target_pairs={{0,112},{16,0},{32,16},{48,32},{64,48},{80,64},{96,80},{112,96},{1... | collective-permute-start | bytes 786440 | tf_op jit(solution)/shard_map/ppermute | solution.py:325
  107.1 8.6 %collective-permute-start.21 = (f32[512,128]{1,0:T(8,128)S(1)}, f32[512,128]{1,0:T(8,128)S(1)}, u32[]{:S(2)}, u32[]{:S(2)}) collective-permute-start(f32[512,128]{1,0:T(8,128)S(1)} %get-tuple-element.55), channel_id=1, source_target_pairs={{0,16},{16,32},{32,48},{48,64},{64,80},{80,96},{96,112},{112,0},{1... | collective-permute-start | bytes 786440 | tf_op jit(solution)/shard_map/ppermute | solution.py:325
  107.1 8.6 %collective-permute-start.22 = (f32[512,128]{1,0:T(8,128)S(1)}, f32[512,128]{1,0:T(8,128)S(1)}, u32[]{:S(2)}, u32[]{:S(2)}) collective-permute-start(f32[512,128]{1,0:T(8,128)S(1)} %get-tuple-element.54), channel_id=1, source_target_pairs={{0,14},{2,0},{4,2},{6,4},{8,6},{10,8},{12,10},{14,12},{1,15},{3,1}... | collective-permute-start | bytes 786440 | tf_op jit(solution)/shard_map/ppermute | solution.py:325
  107.7 8.0 %collective-permute-start.23 = (f32[512,128]{1,0:T(8,128)S(1)}, f32[512,128]{1,0:T(8,128)S(1)}, u32[]{:S(2)}, u32[]{:S(2)}) collective-permute-start(f32[512,128]{1,0:T(8,128)S(1)} %get-tuple-element.53), channel_id=1, source_target_pairs={{0,2},{2,4},{4,6},{6,8},{8,10},{10,12},{12,14},{14,0},{1,3},{3,5},... | collective-permute-start | bytes 786440 | tf_op jit(solution)/shard_map/ppermute | solution.py:325
  119.5 21.6 %copy-start.1 = (f32[6144,128]{1,0:T(8,128)}, f32[6144,128]{1,0:T(8,128)S(1)}, u32[]{:S(2)}) copy-start(f32[6144,128]{1,0:T(8,128)S(1)} %get-tuple-element.42.refs_4_.refs_5_) | copy-start | bytes 9437188
  119.6 4.2 %collective-permute-start.24 = (bf16[512,128]{1,0:T(8,128)(2,1)S(1)}, bf16[512,128]{1,0:T(8,128)(2,1)S(1)}, u32[]{:S(2)}, u32[]{:S(2)}) collective-permute-start(bf16[512,128]{1,0:T(8,128)(2,1)S(1)} %get-tuple-element.68), channel_id=1, source_target_pairs={{0,16},{16,32},{32,48},{48,64},{64,80},{80,96},{96,112},{112,0},{1... | collective-permute-start | bytes 393224 | tf_op jit(solution)/shard_map/ppermute | solution.py:325
  119.7 6.2 %collective-permute-start.25 = (bf16[512,128]{1,0:T(8,128)(2,1)S(1)}, bf16[512,128]{1,0:T(8,128)(2,1)S(1)}, u32[]{:S(2)}, u32[]{:S(2)}) collective-permute-start(bf16[512,128]{1,0:T(8,128)(2,1)S(1)} %get-tuple-element.67), channel_id=1, source_target_pairs={{0,112},{16,0},{32,16},{48,32},{64,48},{80,64},{96,80},{112,96},{1... | collective-permute-start | bytes 393224 | tf_op jit(solution)/shard_map/ppermute | solution.py:325
  121.2 4.6 %collective-permute-start.26 = (bf16[512,128]{1,0:T(8,128)(2,1)S(1)}, bf16[512,128]{1,0:T(8,128)(2,1)S(1)}, u32[]{:S(2)}, u32[]{:S(2)}) collective-permute-start(bf16[512,128]{1,0:T(8,128)(2,1)S(1)} %get-tuple-element.66), channel_id=1, source_target_pairs={{0,2},{2,4},{4,6},{6,8},{8,10},{10,12},{12,14},{14,0},{1,3},{3,5},... | collective-permute-start | bytes 393224 | tf_op jit(solution)/shard_map/ppermute | solution.py:325
  123.8 4.7 %collective-permute-start.27 = (bf16[512,128]{1,0:T(8,128)(2,1)S(1)}, bf16[512,128]{1,0:T(8,128)(2,1)S(1)}, u32[]{:S(2)}, u32[]{:S(2)}) collective-permute-start(bf16[512,128]{1,0:T(8,128)(2,1)S(1)} %get-tuple-element.65), channel_id=1, source_target_pairs={{0,14},{2,0},{4,2},{6,4},{8,6},{10,8},{12,10},{14,12},{1,15},{3,1}... | collective-permute-start | bytes 393224 | tf_op jit(solution)/shard_map/ppermute | solution.py:325
  141.2 2.6 %copy-start.3 = (f32[12296,128]{1,0:T(8,128)}, f32[12296,128]{1,0:T(8,128)S(1)}, u32[]{:S(2)}) copy-start(f32[12296,128]{1,0:T(8,128)S(1)} %get-tuple-element.44.refs_4_) | copy-start | bytes 18886660
  144.9 17.3 %collective-permute-start.28 = (f32[512,128]{1,0:T(8,128)}, f32[512,128]{1,0:T(8,128)S(1)}, u32[]{:S(2)}, u32[]{:S(2)}) collective-permute-start(f32[512,128]{1,0:T(8,128)} %get-tuple-element.52), channel_id=1, source_target_pairs={{0,112},{16,0},{32,16},{48,32},{64,48},{80,64},{96,80},{112,96},{1... | collective-permute-start | bytes 786440 | tf_op jit(solution)/shard_map/ppermute | solution.py:325
  148.5 13.7 %collective-permute-start.29 = (f32[512,128]{1,0:T(8,128)}, f32[512,128]{1,0:T(8,128)}, u32[]{:S(2)}, u32[]{:S(2)}) collective-permute-start(f32[512,128]{1,0:T(8,128)} %get-tuple-element.51), channel_id=1, source_target_pairs={{0,16},{16,32},{32,48},{48,64},{64,80},{80,96},{96,112},{112,0},{1... | collective-permute-start | bytes 786440 | tf_op jit(solution)/shard_map/ppermute | solution.py:325
  148.5 13.7 %collective-permute-start.30 = (f32[512,128]{1,0:T(8,128)}, f32[512,128]{1,0:T(8,128)}, u32[]{:S(2)}, u32[]{:S(2)}) collective-permute-start(f32[512,128]{1,0:T(8,128)} %get-tuple-element.50), channel_id=1, source_target_pairs={{0,14},{2,0},{4,2},{6,4},{8,6},{10,8},{12,10},{14,12},{1,15},{3,1}... | collective-permute-start | bytes 786440 | tf_op jit(solution)/shard_map/ppermute | solution.py:325
  149.2 13.0 %collective-permute-start.31 = (f32[512,128]{1,0:T(8,128)}, f32[512,128]{1,0:T(8,128)}, u32[]{:S(2)}, u32[]{:S(2)}) collective-permute-start(f32[512,128]{1,0:T(8,128)} %get-tuple-element.49), channel_id=1, source_target_pairs={{0,2},{2,4},{4,6},{6,8},{8,10},{10,12},{12,14},{14,0},{1,3},{3,5},... | collective-permute-start | bytes 786440 | tf_op jit(solution)/shard_map/ppermute | solution.py:325
  150.3 1.9 copy-start.2
  152.1 2.8 %copy-start.4 = (f32[12296,128]{1,0:T(8,128)S(1)}, f32[12296,128]{1,0:T(8,128)}, u32[]{:S(2)}) copy-start(f32[12296,128]{1,0:T(8,128)} %copy-done.3) | copy-start | bytes 18886660
  166.9 19.0 %collective-permute-start.32 = (bf16[1536,256]{1,0:T(8,128)(2,1)S(1)}, bf16[1536,256]{1,0:T(8,128)(2,1)S(1)}, u32[]{:S(2)}, u32[]{:S(2)}) collective-permute-start(bf16[1536,256]{1,0:T(8,128)(2,1)S(1)} %get-tuple-element.47), channel_id=1, source_target_pairs={{0,1},{1,0},{2,3},{3,2},{4,5},{5,4},{6,7},{7,6},{8,9},{9,8},{10,11... | collective-permute-start | bytes 2359304 | tf_op jit(solution)/shard_map/ppermute | solution.py:325
  167.2 52.4 %collective-permute-start.33 = (bf16[1536,256]{1,0:T(8,128)(2,1)}, bf16[1536,256]{1,0:T(8,128)(2,1)}, u32[]{:S(2)}, u32[]{:S(2)}) collective-permute-start(bf16[1536,256]{1,0:T(8,128)(2,1)} %get-tuple-element.46), channel_id=1, source_target_pairs={{0,1},{1,0},{2,3},{3,2},{4,5},{5,4},{6,7},{7,6},{8,9},{9,8},{10,11... | collective-permute-start | bytes 2359304 | tf_op jit(solution)/shard_map/ppermute | solution.py:325
  185.9 1.9 copy-start.7
  208.5 0.8 copy-start.6
  209.3 20.7 %all-to-all-start.1 = ((bf16[128,16,128]{2,1,0:T(8,128)(2,1)}), bf16[128,16,128]{2,1,0:T(8,128)(2,1)}, u32[]{:S(2)}, u32[]{:S(2)}) async-start(bf16[128,16,128]{2,1,0:T(8,128)(2,1)} %copy-done.6), calls=%async_computation.1 | async-start | bytes 1048576 | tf_op jit(solution)/shard_map/all_to_all | solution.py:452
  230.0 1.1 copy-start.8
